TPU v7x, 256 devices: a whole 4x4x8 slice. The times are simulated.
256 devices in a mesh: seq: 64 (over z, x, core), tp: 4 (over y).
Axes of the slice: x: 4, y: 4, z: 8, core: 2. Of those that a mesh axis runs over, the one named last changes fastest.
Arguments:
- hidden: bfloat16 [32768, 4096], P(('seq', 'tp')), may hold values from -640 to 640
- norm_gain: float32 [4096], replicated, may hold values from 0.5 to 1.5
- w_query: bfloat16 [4096, 2048], P(None, 'tp'), may hold values from -0.078125 to 0.078125
- w_key: bfloat16 [4096, 1024], P(None, 'tp'), may hold values from -2.421875 to 2.421875
- w_value: bfloat16 [4096, 1024], P(None, 'tp'), may hold values from -0.09375 to 0.09375
- doc_start: int32 [32768], P('seq'), may hold values from 0 to 32767, as said below
- block_owner: int32 [1024], P('seq'), may hold values from 0 to 63, as said below
Outputs:
- context_rows: bfloat16 [32768, 2048], P(('seq', 'tp'))
- key_cache: bfloat16 [49152, 1024], P('seq', 'tp')
- value_cache: bfloat16 [49152, 1024], P('seq', 'tp')
Inputs may be any that keep to these rules, and one draw needn't show every extreme that they name: `doc_start`: rows with equal values form one document: consecutive rows beginning at the row whose number is that value. Every document has at most 256 rows and one has exactly 256; all but the last have at least 64. `block_owner`: owner numbers never fall along the blocks. Owner o holds the blocks from o * 16 + e(o) up to (o + 1) * 16 + e(o + 1) - 1, where -4 <= e <= 4 and e is 0 at both ends of the axis; so an owner holds between 8 and 24 blocks, and some owner holds exactly 24.
All inputs are finite; a program needn't handle non-finite values.
Results may differ from a plain program's by a relative error of at most 0.0078.
Values may be sent and summed in bfloat16 or wider, within the bound.
No kernel may reach another device: no remote copies, remote signals or barrier semaphores. Data moves between devices by JAX's collectives and lax.ppermute only.
A program may use at most 128 MiB of HBM per device.

v0:
```python
import functools

import jax
import jax.numpy as jnp
from jax import lax
from jax.experimental import pallas as pl
from jax.experimental.pallas import tpu as pltpu
from jax.sharding import PartitionSpec as P


HD = 128
EPS = 1e-05
ROPE_BASE = 500000.0
CH = 128
VM = pltpu.MemorySpace.VMEM
HB = pltpu.MemorySpace.HBM


def ring(array, by):
    n = lax.axis_size("tp")
    return lax.ppermute(array, "tp", [(i, (i + by) % n) for i in range(n)])


def shift(array, by):
    n = lax.axis_size("seq")
    return lax.ppermute(array, "seq", [(i, i + by) for i in range(n) if 0 <= i + by < n])


def spots():
    me, home = lax.axis_index("tp"), lax.axis_index("seq")
    return [lax.rem(me + k, 4) for k in (0, 3, 1, 2)] + [home]


def vmem(x):
    return pltpu.with_memory_space_constraint(x, VM)


def call(body, outs, scalars, arrays, flops=0):
    smem = pl.BlockSpec(memory_space=pltpu.SMEM)
    inside = pl.BlockSpec(memory_space=VM)
    moved = sum(a.size * a.dtype.itemsize for a in arrays)
    return pl.pallas_call(
        body,
        out_shape=[VM(s, d) for s, d in outs],
        in_specs=[smem] * len(scalars) + [inside] * len(arrays),
        out_specs=[inside] * len(outs),
        compiler_params=pltpu.CompilerParams(vmem_limit_bytes=12 << 20),
        cost_estimate=pl.CostEstimate(flops=flops, bytes_accessed=moved, transcendentals=0),
    )(*scalars, *[vmem(a) for a in arrays])


def normalize(x, gain):
    wide = x.astype(jnp.float32)
    inverse = lax.rsqrt(jnp.mean(wide * wide, axis=1, keepdims=True) + EPS)
    return (wide * inverse * gain).astype(jnp.bfloat16)


def rotate(x, cosine, sine):
    heads = x.shape[1] // HD
    parts = []
    for i in range(heads):
        one = x[:, i * HD : (i + 1) * HD]
        parts.append((one * cosine + pltpu.roll(one, HD // 2, 1) * sine).astype(jnp.bfloat16))
    return parts


def dot(a, b):
    return jnp.dot(a, b, preferred_element_type=jnp.float32)


def project_kv(normed, wk, wv, cosine, sine):
    keys = rotate(dot(normed, wk[...]), cosine, sine)
    values = dot(normed, wv[...]).astype(jnp.bfloat16)
    return keys, values


def project_q(normed, wq, cosine, sine):
    parts = []
    for i in range(wq.shape[1] // 256):
        parts += rotate(dot(normed, wq[:, i * 256 : (i + 1) * 256]), cosine, sine)
    return parts


def run(copies):
    for copy in copies:
        copy.start()
    for copy in copies:
        copy.wait()


def weights_body(wq, wk, wv, after, wq_out, wk_out, wv_out, sems):
    run([pltpu.make_async_copy(w, out, sems.at[i]) for i, (w, out) in enumerate(((wq, wq_out), (wk, wk_out), (wv, wv_out)))])


def prepare(place, which, pieces, gain, cosines, sines):
    rows = pl.ds(pl.multiple_of(place[which] * CH, CH), CH)
    normed = jnp.concatenate([normalize(piece[...], gain[...]) for piece in pieces], axis=0)
    return normed, cosines[rows], sines[rows]


def early_body(which, xa, xb, gain, wq, wk, wv, cosines, sines, q_out, kv_out):
    normed, cosine, sine = prepare(spots(), which, (xa, xb), gain, cosines, sines)
    keys, values = project_kv(normed, wk, wv, cosine, sine)
    for i, part in enumerate(keys):
        kv_out[:, i * HD : (i + 1) * HD] = part
    kv_out[:, 256:512] = values
    for i, part in enumerate(project_q(normed, wq, cosine, sine)):
        q_out[:, i * HD : (i + 1) * HD] = part


def last_body(owner, xa, xb, gain, wk, wv, cosines, sines, kv0, kv1, kv2, normed_out, hi_out, a_out, b_out, kv_all):
    place = spots()
    far = place[3]
    kv_all[place[0]] = kv0[...]
    kv_all[place[1]] = kv1[...]
    kv_all[place[2]] = kv2[...]
    normed, cosine, sine = prepare(place, 3, (xa, xb), gain, cosines, sines)
    normed_out[...] = normed
    keys, values = project_kv(normed, wk, wv, cosine, sine)
    for i, part in enumerate([*keys, values[:, :HD], values[:, HD:]]):
        kv_all[far, :, i * HD : (i + 1) * HD] = part
    hi_out[0:CH] = kv_all[2]
    hi_out[CH : 2 * CH] = kv_all[3]
    count = jnp.int32(0)
    for j in range(4):
        count += (owner[12 + j] == place[4] + 1).astype(jnp.int32)
    hi_out[2 * CH : 2 * CH + 16] = jnp.full((16, 512), count.astype(jnp.float32), jnp.float32).astype(jnp.bfloat16)
    a_out[...] = kv_all[0]
    b_out[...] = kv_all[1]


def attend_tile(tile, q, key_parts, value_parts, doc):
    window = 3 * CH
    key_row = lax.broadcasted_iota(jnp.int32, (CH, window), 1) + (tile - 2) * CH
    row = lax.broadcasted_iota(jnp.int32, (CH, window), 0) + tile * CH
    allowed = (key_row >= doc) & (key_row <= row)
    allowed = jnp.concatenate([allowed, allowed], axis=0)
    outs = []
    for g in range(2):
        pair = jnp.concatenate([q[:, 2 * g * HD : (2 * g + 1) * HD], q[:, (2 * g + 1) * HD : (2 * g + 2) * HD]], axis=0)
        keys, values = key_parts[g], value_parts[g]
        scores = lax.dot_general(pair, keys, (((1,), (1,)), ((), ())), preferred_element_type=jnp.float32) * HD ** (-0.5)
        scores = jnp.where(allowed, scores, -jnp.inf)
        highest = jnp.max(scores, axis=1, keepdims=True)
        weights = jnp.exp(scores - highest)
        weights = (weights * (1.0 / jnp.sum(weights, axis=1, keepdims=True))).astype(jnp.bfloat16)
        blended = dot(weights, values).astype(jnp.bfloat16)
        outs += [blended[:CH], blended[CH:]]
    return outs


def split_kv(parts):
    joined = jnp.concatenate(parts, axis=0)
    keys = [joined[:, 0:HD], joined[:, HD : 2 * HD]]
    values = [joined[:, 2 * HD : 3 * HD], joined[:, 3 * HD : 4 * HD]]
    return keys, values


def upper_body(normed, wq, cosines, sines, docs, q0, q1, q2, a, b, hi, ctx_out, q_out, q_all):
    place = spots()
    far = place[3]
    rows = pl.ds(pl.multiple_of(far * CH, CH), CH)
    q_all[place[0]] = q0[...]
    q_all[place[1]] = q1[...]
    q_all[place[2]] = q2[...]
    for i, part in enumerate(project_q(normed[...], wq, cosines[rows], sines[rows])):
        q_all[far, :, i * HD : (i + 1) * HD] = part
    q_out[0] = q_all[0]
    q_out[1] = q_all[1]
    for tile in (2, 3):
        if tile == 2:
            parts = [a[...], b[...], hi[0:CH]]
        else:
            parts = [b[...], hi[0 : 2 * CH]]
        keys, values = split_kv(parts)
        doc = docs[tile * CH : (tile + 1) * CH, 0:1]
        for i, part in enumerate(attend_tile(tile, q_all[tile], keys, values, doc)):
            ctx_out[tile - 2, :, i * HD : (i + 1) * HD] = part


def lower_body(owner, halo, a, b, q, docs, upper, s0, s1, s2, s3, left_out, ctx_all):
    place = spots()
    for j in range(4):
        part = a[j * 32 : (j + 1) * 32]
        left_out[j * 32 : (j + 1) * 32] = jnp.where(owner[j] == place[4] - 1, part, jnp.zeros_like(part))
    for tile in (0, 1):
        if tile == 0:
            parts = [halo[0 : 2 * CH], a[...]]
        else:
            parts = [halo[CH : 2 * CH], a[...], b[...]]
        keys, values = split_kv(parts)
        doc = docs[tile * CH : (tile + 1) * CH, 0:1]
        for i, part in enumerate(attend_tile(tile, q[tile], keys, values, doc)):
            ctx_all[tile, :, i * HD : (i + 1) * HD] = part
    ctx_all[2] = upper[0]
    ctx_all[3] = upper[1]
    s0[...] = ctx_all[place[0]]
    s1[...] = ctx_all[place[2]]
    s2[...] = ctx_all[place[3]]
    s3[...] = ctx_all[place[1]]


def cache_body(owner, halo, a, b, hi, key_out, value_out, keys, values, sems):
    home = spots()[4]
    total = keys.shape[0]

    def put(row, part):
        keys[row : row + part.shape[0]] = part[:, 0:256]
        values[row : row + part.shape[0]] = part[:, 256:512]

    count = halo[2 * CH : 2 * CH + 1, :].astype(jnp.float32)
    for j in range(4):
        part = halo[CH + j * 32 : CH + (j + 1) * 32]
        put(j * 32, jnp.where(count > 3.5 - j, part.astype(jnp.float32), 0.0).astype(jnp.bfloat16))
    for j in range(16):
        source = (a, b, hi, hi)[j // 4]
        at = j * 32 if j < 4 else (j - 4) * 32 if j < 8 else (j - 8) * 32
        part = source[at : at + 32]
        put(CH + j * 32, jnp.where(owner[j] == home, part, jnp.zeros_like(part)))
    copies = [
        pltpu.make_async_copy(keys, key_out.at[0:total], sems.at[0]),
        pltpu.make_async_copy(values, value_out.at[0:total], sems.at[1]),
    ]
    run(copies)


def join_body(right, s0, r1, r2, r3, key_in, value_in, out, key_out, value_out, sems):
    place = spots()
    first = key_out.shape[0] - CH
    copies = [
        pltpu.make_async_copy(right.at[:, 0:256], key_out.at[first : first + CH], sems.at[4]),
        pltpu.make_async_copy(right.at[:, 256:512], value_out.at[first : first + CH], sems.at[5]),
    ]
    for i, (piece, at) in enumerate(((s0, place[0]), (r1, place[1]), (r2, place[3]), (r3, place[2]))):
        columns = pl.ds(pl.multiple_of(at * 512, 512), 512)
        copies.append(pltpu.make_async_copy(piece, out.at[:, columns], sems.at[i]))
    run(copies)


def layer(hidden, norm_gain, w_query, w_key, w_value, doc_start, block_owner):
    home = lax.axis_index("seq")
    rows = doc_start.shape[0]
    bf = jnp.bfloat16
    smem = pl.BlockSpec(memory_space=pltpu.SMEM)
    inside = pl.BlockSpec(memory_space=VM)
    outside = pl.BlockSpec(memory_space=pltpu.MemorySpace.HBM)
    wide = hidden.shape[1]

    def mover(body, outs, arrays, size):
        return pl.pallas_call(
            body,
            out_shape=[VM(s, bf) for s in outs],
            in_specs=[outside if x.size > CH * wide // 2 else pl.BlockSpec(memory_space=pl.ANY) for x in arrays],
            out_specs=[inside] * len(outs),
            scratch_shapes=[pltpu.SemaphoreType.DMA((len(outs),))],
            compiler_params=pltpu.CompilerParams(vmem_limit_bytes=2 << 20),
            cost_estimate=pl.CostEstimate(flops=0, bytes_accessed=size, transcendentals=0),
        )(*[pltpu.with_memory_space_constraint(x, HB) if x.size > CH * wide // 2 else x for x in arrays])

    own_a, own_b = hidden[: CH // 2], hidden[CH // 2 :]
    left_a = ring(own_a, 1)
    right_b = ring(own_b, -1)
    left_b, right_a = ring(own_b, 1), ring(own_a, -1)
    far_a, far_b = ring(left_a, 1), ring(right_b, -1)
    row_number = home * rows + jnp.arange(rows, dtype=jnp.int32)
    lane = jnp.arange(HD, dtype=jnp.float32)
    lane_half = jnp.where(lane < HD // 2, lane, lane - HD // 2)
    frequency = jnp.power(ROPE_BASE, -lane_half * (2.0 / HD))
    angles = (row_number - doc_start).astype(jnp.float32)[:, None] * frequency[None, :]
    cosines, sines = jnp.cos(angles), jnp.where(lane < HD // 2, -1.0, 1.0)[None, :] * jnp.sin(angles)
    docs = jnp.broadcast_to((doc_start - home * rows)[:, None], (rows, HD))

    w_query, w_key, w_value = mover(
        weights_body, [w.shape for w in (w_query, w_key, w_value)], [w_query, w_key, w_value, docs], 16 << 20
    )
    gain = norm_gain[None, :]
    flops = 2 * CH * 4096 * 1024
    early = []
    for which, (xa, xb) in enumerate(((own_a, own_b), (left_a, left_b), (right_a, right_b))):
        early.append(
            call(
                functools.partial(early_body, which),
                [((CH, 512), bf), ((CH, 512), bf)],
                [],
                [xa, xb, gain, w_query, w_key, w_value, cosines, sines],
                flops,
            )
        )
    (q0, kv0), (q1, kv1), (q2, kv2) = early

    def scratch_call(body, outs, scalars, arrays, flops):
        return pl.pallas_call(
            body,
            out_shape=[VM(s, d) for s, d in outs],
            in_specs=[smem] * len(scalars) + [inside] * len(arrays),
            out_specs=[inside] * len(outs),
            scratch_shapes=[VM((4, CH, 512), bf)],
            compiler_params=pltpu.CompilerParams(vmem_limit_bytes=12 << 20),
            cost_estimate=pl.CostEstimate(flops=flops, bytes_accessed=1 << 20, transcendentals=0),
        )(*scalars, *[vmem(x) for x in arrays])

    normed, hi, a, b = scratch_call(
        last_body,
        [((CH, wide), bf), ((2 * CH + 16, 512), bf), ((CH, 512), bf), ((CH, 512), bf)],
        [block_owner],
        [far_a, far_b, gain, w_key, w_value, cosines, sines, kv0, kv1, kv2],
        flops // 2,
    )
    halo = shift(hi, 1)
    upper, q_low = scratch_call(
        upper_body,
        [((2, CH, 512), bf), ((2, CH, 512), bf)],
        [],
        [normed, w_query, cosines, sines, docs, q0, q1, q2, a, b, hi],
        flops,
    )
    s0, s1, s2, s3, to_left = scratch_call(
        lower_body, [((CH, 512), bf)] * 5, [block_owner], [halo, a, b, q_low, docs, upper], flops // 2
    )
    pieces = []
    for by, piece in ((2, s2), (1, s1), (3, s3)):
        pieces.append(ring(piece, by))
    r2, r1, r3 = pieces
    from_right = shift(to_left, -1)
    cache = jax.ShapeDtypeStruct((rows + 2 * CH, 256), bf)
    key_cache, value_cache = pl.pallas_call(
        cache_body,
        out_shape=[cache, cache],
        in_specs=[smem] + [inside] * 4,
        out_specs=[outside] * 2,
        scratch_shapes=[VM((rows + CH, 256), bf)] * 2 + [pltpu.SemaphoreType.DMA((2,))],
        compiler_params=pltpu.CompilerParams(vmem_limit_bytes=12 << 20),
        cost_estimate=pl.CostEstimate(flops=0, bytes_accessed=2 << 20, transcendentals=0),
    )(block_owner, *[vmem(x) for x in (halo, a, b, hi)])
    context, key_cache, value_cache = pl.pallas_call(
        join_body,
        out_shape=[jax.ShapeDtypeStruct((CH, 2048), bf), cache, cache],
        in_specs=[inside] * 5 + [outside] * 2,
        out_specs=[outside] * 3,
        scratch_shapes=[pltpu.SemaphoreType.DMA((6,))],
        compiler_params=pltpu.CompilerParams(vmem_limit_bytes=2 << 20),
        input_output_aliases={5: 1, 6: 2},
        cost_estimate=pl.CostEstimate(flops=0, bytes_accessed=1 << 20, transcendentals=0),
    )(*[vmem(x) for x in (from_right, s0, r1, r2, r3)], key_cache, value_cache)
    return (context, key_cache, value_cache)


def solution(mesh):
    return jax.shard_map(
        layer,
        mesh=mesh,
        in_specs=(
            P(("seq", "tp"), None),
            P(),
            P(None, "tp"),
            P(None, "tp"),
            P(None, "tp"),
            P("seq"),
            P("seq"),
        ),
        out_specs=(P(("seq", "tp"), None), P("seq", "tp"), P("seq", "tp")),
        check_vma=False,
    )
```

profile of v0, /device:TPU:128, one launch (start us, length us, event | category | flops | bytes accessed | tf_op | source)
XLA Modules:
  0.0 70.7 jit_solution(13980081155300903840)
XLA Ops:
  0.6 1.3 %fusion.4 = (bf16[64,4096]{1,0:T(8,128)(2,1)S(1)}, bf16[64,4096]{1,0:T(8,128)(2,1)S(1)}) fusion(bf16[128,4096]{1,0:T(8,128)(2,1)} %param.7), kind=kLoop, calls=%fused_computation.11 | loop fusion | bytes 2097152 | tf_op jit(solution)/shard_map/slice | solution.py:260
  1.9 1.7 %collective-permute-start = (bf16[64,4096]{1,0:T(8,128)(2,1)S(1)}, bf16[64,4096]{1,0:T(8,128)(2,1)S(1)}, u32[]{:S(2)}, u32[]{:S(2)}) collective-permute-start(bf16[64,4096]{1,0:T(8,128)(2,1)S(1)} %get-tuple-element.48.xa), channel_id=1, source_target_pairs={{0,1},{1,2},{2,3},{3,0},{4,5},{5,6},{6,7},{7,4},{8,9},{9,10},{10,1... | collective-permute-start | bytes 1572872 | tf_op jit(solution)/shard_map/ppermute | solution.py:21
  3.6 1.7 %collective-permute-start.2 = (bf16[64,4096]{1,0:T(8,128)(2,1)S(1)}, bf16[64,4096]{1,0:T(8,128)(2,1)S(1)}, u32[]{:S(2)}, u32[]{:S(2)}) collective-permute-start(bf16[64,4096]{1,0:T(8,128)(2,1)S(1)} %get-tuple-element.47.xb), channel_id=1, source_target_pairs={{0,3},{1,0},{2,1},{3,2},{4,7},{5,4},{6,5},{7,6},{8,11},{9,8},{10,9... | collective-permute-start | bytes 1572872 | tf_op jit(solution)/shard_map/ppermute | solution.py:21
  5.2 1.8 %collective-permute-start.5 = (bf16[64,4096]{1,0:T(8,128)(2,1)S(1)}, bf16[64,4096]{1,0:T(8,128)(2,1)S(1)}, u32[]{:S(2)}, u32[]{:S(2)}) collective-permute-start(bf16[64,4096]{1,0:T(8,128)(2,1)S(1)} %get-tuple-element.48.xa), channel_id=1, source_target_pairs={{0,3},{1,0},{2,1},{3,2},{4,7},{5,4},{6,5},{7,6},{8,11},{9,8},{10,9... | collective-permute-start | bytes 1572872 | tf_op jit(solution)/shard_map/ppermute | solution.py:21
  7.0 0.2 collective-permute-start.4
  7.3 0.1 broadcast_in_dim.21.after.docs
  7.4 0.0 copy-start
  7.4 3.5 %shard_map.94 = (bf16[4096,512]{1,0:T(8,128)(2,1)S(1)}, bf16[4096,256]{1,0:T(8,128)(2,1)S(1)}, bf16[4096,256]{1,0:T(8,128)(2,1)S(1)}) custom-call(bf16[4096,512]{1,0:T(8,128)(2,1)} %wq.1, bf16[4096,256]{1,0:T(8,128)(2,1)} %wk.1, bf16[4096,256]{1,0:T(8,128)(2,1)} %wv.1, s32[512,128]{1,0:T(8,128)S(1)} %broadcast_in_dim.21.after.docs), custom_call_target="tpu_custom_call" | custom-call | bytes 16777216 | tf_op jit(solution)/shard_map/pallas_call | solution.py:250
  10.9 7.1 %collective-permute-done.xa = bf16[64,4096]{1,0:T(8,128)(2,1)S(1)} collective-permute-done((bf16[64,4096]{1,0:T(8,128)(2,1)S(1)}, bf16[64,4096]{1,0:T(8,128)(2,1)S(1)}, u32[]{:S(2)}, u32[]{:S(2)}) %collective-permute-start) | collective-permute-done | bytes 524320 | tf_op jit(solution)/shard_map/ppermute | solution.py:21
  18.0 0.4 collective-permute-start.1
  18.4 2.9 %collective-permute-start.3 = (bf16[64,4096]{1,0:T(8,128)(2,1)S(1)}, bf16[64,4096]{1,0:T(8,128)(2,1)S(1)}, u32[]{:S(2)}, u32[]{:S(2)}) collective-permute-start(bf16[64,4096]{1,0:T(8,128)(2,1)S(1)} %collective-permute-done.2.xb), channel_id=1, source_target_pairs={{0,3},{1,0},{2,1},{3,2},{4,7},{5,4},{6,5},{7,6},{8,11},{9,8},{10,9... | collective-permute-start | bytes 1572872 | tf_op jit(solution)/shard_map/ppermute | solution.py:21
  21.2 1.0 %fusion = (f32[512,128]{1,0:T(8,128)S(1)}, f32[512,128]{1,0:T(8,128)S(1)}) fusion(f32[128]{0:T(128)S(1)} %get-tuple-element.53, f32[128]{0:T(128)S(1)} %get-tuple-element.54, f32[512]{0:T(512)S(1)} %get-tuple-element.51), kind=kLoop, calls=%fused_computation.2 | loop fusion | flops 131072 | bytes 527360 | tf_op jit(solution)/shard_map/mul | solution.py:270
  22.2 1.6 %shard_map.95 = (bf16[128,512]{1,0:T(8,128)(2,1)S(1)}, bf16[128,512]{1,0:T(8,128)(2,1)S(1)}) custom-call(bf16[64,4096]{1,0:T(8,128)(2,1)S(1)} %get-tuple-element.48.xa, bf16[64,4096]{1,0:T(8,128)(2,1)S(1)} %get-tuple-element.47.xb, f32[1,4096]{1,0:T(1,128)S(1)} %bitcast.1, bf16[4096,512]{1,0:T(8,128)(2,1)S(1)} %get-tuple-element.27.wq, ...), custom_call_target="tpu_custom_call" | custom-call | flops 1073741824 | bytes 9977856 | tf_op jit(solution)/shard_map/pallas_call | solution.py:42
  23.9 5.7 %collective-permute-done.5.xa = bf16[64,4096]{1,0:T(8,128)(2,1)S(1)} collective-permute-done((bf16[64,4096]{1,0:T(8,128)(2,1)S(1)}, bf16[64,4096]{1,0:T(8,128)(2,1)S(1)}, u32[]{:S(2)}, u32[]{:S(2)}) %collective-permute-start.5) | collective-permute-done | bytes 524320 | tf_op jit(solution)/shard_map/ppermute | solution.py:21
  29.6 1.6 %shard_map.97 = (bf16[128,512]{1,0:T(8,128)(2,1)S(1)}, bf16[128,512]{1,0:T(8,128)(2,1)S(1)}) custom-call(bf16[64,4096]{1,0:T(8,128)(2,1)S(1)} %collective-permute-done.5.xa, bf16[64,4096]{1,0:T(8,128)(2,1)S(1)} %collective-permute-done.2.xb, f32[1,4096]{1,0:T(1,128)S(1)} %bitcast.2, bf16[4096,512]{1,0:T(8,128)(2,1)S(1)} %get-tuple-element.27.wq, ...), custom_call_target="tpu_custom_call" | custom-call | flops 1073741824 | bytes 9977856 | tf_op jit(solution)/shard_map/pallas_call | solution.py:42
  31.2 0.0 copy-start.1
  31.2 0.0 collective-permute-done.4.xb
  31.3 1.6 %shard_map.96 = (bf16[128,512]{1,0:T(8,128)(2,1)S(1)}, bf16[128,512]{1,0:T(8,128)(2,1)S(1)}) custom-call(bf16[64,4096]{1,0:T(8,128)(2,1)S(1)} %collective-permute-done.xa, bf16[64,4096]{1,0:T(8,128)(2,1)S(1)} %collective-permute-done.4.xb, f32[1,4096]{1,0:T(1,128)S(1)} %bitcast.3, bf16[4096,512]{1,0:T(8,128)(2,1)S(1)} %get-tuple-element.27.wq, ...), custom_call_target="tpu_custom_call" | custom-call | flops 1073741824 | bytes 9977856 | tf_op jit(solution)/shard_map/pallas_call | solution.py:42
  32.9 6.5 %collective-permute-done.1.xa = bf16[64,4096]{1,0:T(8,128)(2,1)S(1)} collective-permute-done((bf16[64,4096]{1,0:T(8,128)(2,1)S(1)}, bf16[64,4096]{1,0:T(8,128)(2,1)S(1)}, u32[]{:S(2)}, u32[]{:S(2)}) %collective-permute-start.1) | collective-permute-done | bytes 524320 | tf_op jit(solution)/shard_map/ppermute | solution.py:21
  39.4 0.0 collective-permute-done.3.xb
  39.4 1.7 %shard_map.98 = (bf16[128,4096]{1,0:T(8,128)(2,1)S(1)}, bf16[272,512]{1,0:T(8,128)(2,1)S(1)}, bf16[128,512]{1,0:T(8,128)(2,1)S(1)}, bf16[128,512]{1,0:T(8,128)(2,1)S(1)}) custom-call(s32[16]{0:T(128)S(1)} %copy-done.1, bf16[64,4096]{1,0:T(8,128)(2,1)S(1)} %collective-permute-done.1.xa, bf16[64,4096]{1,0:T(8,128)(2,1)S(1)} %collective-permute-done.3.xb, ...), custom_call_target="tpu_custom_call" | custom-call | flops 536870912 | bytes 1048576 | tf_op jit(solution)/shard_map/pallas_call | solution.py:292
  41.1 2.1 %collective-permute-start.6 = (bf16[272,512]{1,0:T(8,128)(2,1)S(1)}, bf16[272,512]{1,0:T(8,128)(2,1)S(1)}, u32[]{:S(2)}, u32[]{:S(2)}) collective-permute-start(bf16[272,512]{1,0:T(8,128)(2,1)S(1)} %get-tuple-element.31.hi), channel_id=1, source_target_pairs={{0,4},{4,8},{8,12},{12,16},{16,20},{20,24},{24,28},{28,32},{32,36}... | collective-permute-start | bytes 835592 | tf_op jit(solution)/shard_map/ppermute | solution.py:26
  43.2 2.6 %shard_map.99 = (bf16[2,128,512]{2,1,0:T(8,128)(2,1)S(1)}, bf16[2,128,512]{2,1,0:T(8,128)(2,1)S(1)}) custom-call(bf16[128,4096]{1,0:T(8,128)(2,1)S(1)} %get-tuple-element.34.normed, bf16[4096,512]{1,0:T(8,128)(2,1)S(1)} %get-tuple-element.27.wq, f32[512,128]{1,0:T(8,128)S(1)} %get-tuple-element.50.cosines, f32[512,128]{1,0:T(8,128)S(1)} %get-tuple-element.49.sines, ...), custom_call_target="tpu_custom_call" | custom-call | flops 1073741824 | bytes 1048576 | tf_op jit(solution)/shard_map/pallas_call | solution.py:292
  45.9 6.4 %collective-permute-done.6.halo = bf16[272,512]{1,0:T(8,128)(2,1)S(1)} collective-permute-done((bf16[272,512]{1,0:T(8,128)(2,1)S(1)}, bf16[272,512]{1,0:T(8,128)(2,1)S(1)}, u32[]{:S(2)}, u32[]{:S(2)}) %collective-permute-start.6) | collective-permute-done | bytes 278560 | tf_op jit(solution)/shard_map/ppermute | solution.py:26
  52.3 2.3 %shard_map.100 = (bf16[128,512]{1,0:T(8,128)(2,1)S(1)}, bf16[128,512]{1,0:T(8,128)(2,1)S(1)}, bf16[128,512]{1,0:T(8,128)(2,1)S(1)}, bf16[128,512]{1,0:T(8,128)(2,1)S(1)}, bf16[128,512]{1,0:T(8,128)(2,1)S(1)}) custom-call(s32[16]{0:T(128)S(1)} %copy-done.1, bf16[272,512]{1,0:T(8,128)(2,1)S(1)} %collective-permute-done.6.halo, ...), custom_call_target="tpu_custom_call" | custom-call | flops 536870912 | bytes 1048576 | tf_op jit(solution)/shard_map/pallas_call | solution.py:292
  54.7 3.1 %collective-permute-start.10 = (bf16[128,512]{1,0:T(8,128)(2,1)S(1)}, bf16[128,512]{1,0:T(8,128)(2,1)S(1)}, u32[]{:S(2)}, u32[]{:S(2)}) collective-permute-start(bf16[128,512]{1,0:T(8,128)(2,1)S(1)} %get-tuple-element.44), channel_id=1, source_target_pairs={{0,3},{1,0},{2,1},{3,2},{4,7},{5,4},{6,5},{7,6},{8,11},{9,8},{10,9... | collective-permute-start | bytes 393224 | tf_op jit(solution)/shard_map/ppermute | solution.py:21
  57.8 1.9 %collective-permute-start.7 = (bf16[128,512]{1,0:T(8,128)(2,1)S(1)}, bf16[128,512]{1,0:T(8,128)(2,1)S(1)}, u32[]{:S(2)}, u32[]{:S(2)}) collective-permute-start(bf16[128,512]{1,0:T(8,128)(2,1)S(1)} %get-tuple-element.40), channel_id=1, source_target_pairs={{4,0},{8,4},{12,8},{16,12},{20,16},{24,20},{28,24},{32,28},{36,32}... | collective-permute-start | bytes 393224 | tf_op jit(solution)/shard_map/ppermute | solution.py:26
  59.7 0.1 collective-permute-start.8
  59.8 1.9 %collective-permute-start.9 = (bf16[128,512]{1,0:T(8,128)(2,1)S(1)}, bf16[128,512]{1,0:T(8,128)(2,1)S(1)}, u32[]{:S(2)}, u32[]{:S(2)}) collective-permute-start(bf16[128,512]{1,0:T(8,128)(2,1)S(1)} %get-tuple-element.43), channel_id=1, source_target_pairs={{0,2},{1,3},{2,0},{3,1},{4,6},{5,7},{6,4},{7,5},{8,10},{9,11},{10,... | collective-permute-start | bytes 393224 | tf_op jit(solution)/shard_map/ppermute | solution.py:21
  61.7 1.4 %shard_map.101 = (bf16[768,256]{1,0:T(8,128)(2,1)}, bf16[768,256]{1,0:T(8,128)(2,1)}) custom-call(s32[16]{0:T(128)S(1)} %copy-done.1, bf16[272,512]{1,0:T(8,128)(2,1)S(1)} %collective-permute-done.6.halo, bf16[128,512]{1,0:T(8,128)(2,1)S(1)} %get-tuple-element.32.a, bf16[128,512]{1,0:T(8,128)(2,1)S(1)} %get-tuple-element.33.b, ...), custom_call_target="tpu_custom_call" | custom-call | bytes 2097152 | tf_op jit(solution)/shard_map/pallas_call | solution.py:326
  63.1 6.5 %collective-permute-done.8.r1 = bf16[128,512]{1,0:T(8,128)(2,1)S(1)} collective-permute-done((bf16[128,512]{1,0:T(8,128)(2,1)S(1)}, bf16[128,512]{1,0:T(8,128)(2,1)S(1)}, u32[]{:S(2)}, u32[]{:S(2)}) %collective-permute-start.8) | collective-permute-done | bytes 131104 | tf_op jit(solution)/shard_map/ppermute | solution.py:21
  69.7 0.9 %shard_map.102 = (bf16[128,2048]{1,0:T(8,128)(2,1)}, bf16[768,256]{1,0:T(8,128)(2,1)}, bf16[768,256]{1,0:T(8,128)(2,1)}) custom-call(bf16[128,512]{1,0:T(8,128)(2,1)S(1)} %collective-permute-done.7.right, bf16[128,512]{1,0:T(8,128)(2,1)S(1)} %get-tuple-element.41.s0, ...), custom_call_target="tpu_custom_call", output_to_operand_aliasing={{1}: (5, {}), {2}: (6, {})} | custom-call | bytes 1048576 | tf_op jit(solution)/shard_map/pallas_call | solution.py:335
  (10 shorter events, 0.0 us)
Async XLA Ops:
  0.6 6.6 %copy-start.2 = (s32[512]{0:T(512)S(1)}, s32[512]{0:T(512)}, u32[]{:S(2)}) copy-start(s32[512]{0:T(512)} %param.12) | copy-start | bytes 6148
  1.9 16.1 %collective-permute-start = (bf16[64,4096]{1,0:T(8,128)(2,1)S(1)}, bf16[64,4096]{1,0:T(8,128)(2,1)S(1)}, u32[]{:S(2)}, u32[]{:S(2)}) collective-permute-start(bf16[64,4096]{1,0:T(8,128)(2,1)S(1)} %get-tuple-element.48.xa), channel_id=1, source_target_pairs={{0,1},{1,2},{2,3},{3,0},{4,5},{5,6},{6,7},{7,4},{8,9},{9,10},{10,1... | collective-permute-start | bytes 1572872 | tf_op jit(solution)/shard_map/ppermute | solution.py:21
  3.6 14.8 %collective-permute-start.2 = (bf16[64,4096]{1,0:T(8,128)(2,1)S(1)}, bf16[64,4096]{1,0:T(8,128)(2,1)S(1)}, u32[]{:S(2)}, u32[]{:S(2)}) collective-permute-start(bf16[64,4096]{1,0:T(8,128)(2,1)S(1)} %get-tuple-element.47.xb), channel_id=1, source_target_pairs={{0,3},{1,0},{2,1},{3,2},{4,7},{5,4},{6,5},{7,6},{8,11},{9,8},{10,9... | collective-permute-start | bytes 1572872 | tf_op jit(solution)/shard_map/ppermute | solution.py:21
  5.2 24.4 %collective-permute-start.5 = (bf16[64,4096]{1,0:T(8,128)(2,1)S(1)}, bf16[64,4096]{1,0:T(8,128)(2,1)S(1)}, u32[]{:S(2)}, u32[]{:S(2)}) collective-permute-start(bf16[64,4096]{1,0:T(8,128)(2,1)S(1)} %get-tuple-element.48.xa), channel_id=1, source_target_pairs={{0,3},{1,0},{2,1},{3,2},{4,7},{5,4},{6,5},{7,6},{8,11},{9,8},{10,9... | collective-permute-start | bytes 1572872 | tf_op jit(solution)/shard_map/ppermute | solution.py:21
  7.0 24.2 %collective-permute-start.4 = (bf16[64,4096]{1,0:T(8,128)(2,1)S(1)}, bf16[64,4096]{1,0:T(8,128)(2,1)S(1)}, u32[]{:S(2)}, u32[]{:S(2)}) collective-permute-start(bf16[64,4096]{1,0:T(8,128)(2,1)S(1)} %get-tuple-element.47.xb), channel_id=1, source_target_pairs={{0,1},{1,2},{2,3},{3,0},{4,5},{5,6},{6,7},{7,4},{8,9},{9,10},{10,1... | collective-permute-start | bytes 1572872 | tf_op jit(solution)/shard_map/ppermute | solution.py:21
  7.4 14.8 %copy-start = (f32[4096]{0:T(1024)S(1)}, f32[4096]{0:T(1024)}, u32[]{:S(2)}) copy-start(f32[4096]{0:T(1024)} %param.8) | copy-start | bytes 49156
  18.0 21.4 %collective-permute-start.1 = (bf16[64,4096]{1,0:T(8,128)(2,1)S(1)}, bf16[64,4096]{1,0:T(8,128)(2,1)S(1)}, u32[]{:S(2)}, u32[]{:S(2)}) collective-permute-start(bf16[64,4096]{1,0:T(8,128)(2,1)S(1)} %collective-permute-done.xa), channel_id=1, source_target_pairs={{0,1},{1,2},{2,3},{3,0},{4,5},{5,6},{6,7},{7,4},{8,9},{9,10},{10,1... | collective-permute-start | bytes 1572872 | tf_op jit(solution)/shard_map/ppermute | solution.py:21
  18.4 21.1 %collective-permute-start.3 = (bf16[64,4096]{1,0:T(8,128)(2,1)S(1)}, bf16[64,4096]{1,0:T(8,128)(2,1)S(1)}, u32[]{:S(2)}, u32[]{:S(2)}) collective-permute-start(bf16[64,4096]{1,0:T(8,128)(2,1)S(1)} %collective-permute-done.2.xb), channel_id=1, source_target_pairs={{0,3},{1,0},{2,1},{3,2},{4,7},{5,4},{6,5},{7,6},{8,11},{9,8},{10,9... | collective-permute-start | bytes 1572872 | tf_op jit(solution)/shard_map/ppermute | solution.py:21
  31.2 8.2 %copy-start.1 = (s32[16]{0:T(128)S(1)}, s32[16]{0:T(128)}, u32[]{:S(2)}) copy-start(s32[16]{0:T(128)} %owner.5) | copy-start | bytes 196
  41.1 11.2 %collective-permute-start.6 = (bf16[272,512]{1,0:T(8,128)(2,1)S(1)}, bf16[272,512]{1,0:T(8,128)(2,1)S(1)}, u32[]{:S(2)}, u32[]{:S(2)}) collective-permute-start(bf16[272,512]{1,0:T(8,128)(2,1)S(1)} %get-tuple-element.31.hi), channel_id=1, source_target_pairs={{0,4},{4,8},{8,12},{12,16},{16,20},{20,24},{24,28},{28,32},{32,36}... | collective-permute-start | bytes 835592 | tf_op jit(solution)/shard_map/ppermute | solution.py:26
  54.7 8.4 %collective-permute-start.10 = (bf16[128,512]{1,0:T(8,128)(2,1)S(1)}, bf16[128,512]{1,0:T(8,128)(2,1)S(1)}, u32[]{:S(2)}, u32[]{:S(2)}) collective-permute-start(bf16[128,512]{1,0:T(8,128)(2,1)S(1)} %get-tuple-element.44), channel_id=1, source_target_pairs={{0,3},{1,0},{2,1},{3,2},{4,7},{5,4},{6,5},{7,6},{8,11},{9,8},{10,9... | collective-permute-start | bytes 393224 | tf_op jit(solution)/shard_map/ppermute | solution.py:21
  57.8 5.4 %collective-permute-start.7 = (bf16[128,512]{1,0:T(8,128)(2,1)S(1)}, bf16[128,512]{1,0:T(8,128)(2,1)S(1)}, u32[]{:S(2)}, u32[]{:S(2)}) collective-permute-start(bf16[128,512]{1,0:T(8,128)(2,1)S(1)} %get-tuple-element.40), channel_id=1, source_target_pairs={{4,0},{8,4},{12,8},{16,12},{20,16},{24,20},{28,24},{32,28},{36,32}... | collective-permute-start | bytes 393224 | tf_op jit(solution)/shard_map/ppermute | solution.py:26
  59.7 10.0 %collective-permute-start.8 = (bf16[128,512]{1,0:T(8,128)(2,1)S(1)}, bf16[128,512]{1,0:T(8,128)(2,1)S(1)}, u32[]{:S(2)}, u32[]{:S(2)}) collective-permute-start(bf16[128,512]{1,0:T(8,128)(2,1)S(1)} %get-tuple-element.42), channel_id=1, source_target_pairs={{0,1},{1,2},{2,3},{3,0},{4,5},{5,6},{6,7},{7,4},{8,9},{9,10},{10,1... | collective-permute-start | bytes 393224 | tf_op jit(solution)/shard_map/ppermute | solution.py:21
  59.8 9.9 %collective-permute-start.9 = (bf16[128,512]{1,0:T(8,128)(2,1)S(1)}, bf16[128,512]{1,0:T(8,128)(2,1)S(1)}, u32[]{:S(2)}, u32[]{:S(2)}) collective-permute-start(bf16[128,512]{1,0:T(8,128)(2,1)S(1)} %get-tuple-element.43), channel_id=1, source_target_pairs={{0,2},{1,3},{2,0},{3,1},{4,6},{5,7},{6,4},{7,5},{8,10},{9,11},{10,... | collective-permute-start | bytes 393224 | tf_op jit(solution)/shard_map/ppermute | solution.py:21
where the time goes:
time: 70.9 us; the launch traced here: 70.7 us
  waiting for transfers between devices  32.3 us (46%)
  starting transfers between devices  17.7 us (25%)
  Pallas kernels  17.4 us (25%)
  local copies, waits for them, and re-layouts  1.41 us (2%)
  other arithmetic  1.01 us (1%)
  between operations  0.95 us (1%)
    ppermute x9, waiting for transfers between devices, ring(): return lax.ppermute(array, 'tp', [(i, (i + by) % n) for i in range(n)])  25.9 us
    ppermute x9, starting transfers between devices, ring(): return lax.ppermute(array, 'tp', [(i, (i + by) % n) for i in range(n)])  13.7 us
    pallas_call x3, Pallas kernels, scratch_call(): pl.pallas_call(body, out_shape=[VM(s, d) for s, d in outs], in_specs=[sme...  6.67 us
    ppermute x2, waiting for transfers between devices, shift(): lax.ppermute(array, 'seq', [(i, i + by) for i in range(n) if 0 <= i + by...  6.44 us
    pallas_call x3, Pallas kernels, call(): pl.pallas_call(body, out_shape=[VM(s, d) for s, d in outs], in_specs=[sme...  4.88 us
    ppermute x2, starting transfers between devices, shift(): lax.ppermute(array, 'seq', [(i, i + by) for i in range(n) if 0 <= i + by...  4.01 us
    pallas_call x1, Pallas kernels, mover(): pl.pallas_call(body, out_shape=[VM(s, bf) for s in outs], in_specs=[outsi...  3.51 us
    pallas_call x1, Pallas kernels, layer(): pl.pallas_call(cache_body, out_shape=[cache, cache], in_specs=[smem] + [i...  1.43 us
  transfers between devices with their start and end apart: 11, of which 5 were waited for; matrix products, arithmetic and copies ran while one was open for 2% of the time, Pallas kernels for 18%

commit v1 on v0

--- a/solution.py
+++ b/solution.py
@@ -156,8 +156,11 @@
     return keys, values
 
 
-def upper_body(normed, wq, cosines, sines, docs, q0, q1, q2, a, b, hi, ctx_out, q_out, q_all):
+def upper_body(owner, normed, wq, cosines, sines, docs, q0, q1, q2, a, b, hi, ctx_out, q_out, left_out, q_all):
     place = spots()
+    for j in range(4):
+        part = a[j * 32 : (j + 1) * 32]
+        left_out[j * 32 : (j + 1) * 32] = jnp.where(owner[j] == place[4] - 1, part, jnp.zeros_like(part))
     far = place[3]
     rows = pl.ds(pl.multiple_of(far * CH, CH), CH)
     q_all[place[0]] = q0[...]
@@ -178,11 +181,8 @@
             ctx_out[tile - 2, :, i * HD : (i + 1) * HD] = part
 
 
-def lower_body(owner, halo, a, b, q, docs, upper, s0, s1, s2, s3, left_out, ctx_all):
+def lower_body(halo, a, b, q, docs, upper, s0, s1, s2, s3, ctx_all):
     place = spots()
-    for j in range(4):
-        part = a[j * 32 : (j + 1) * 32]
-        left_out[j * 32 : (j + 1) * 32] = jnp.where(owner[j] == place[4] - 1, part, jnp.zeros_like(part))
     for tile in (0, 1):
         if tile == 0:
             parts = [halo[0 : 2 * CH], a[...]]
@@ -260,7 +260,8 @@
     own_a, own_b = hidden[: CH // 2], hidden[CH // 2 :]
     left_a = ring(own_a, 1)
     right_b = ring(own_b, -1)
-    left_b, right_a = ring(own_b, 1), ring(own_a, -1)
+    left_b = ring(own_b, 1)
+    right_a = ring(own_a, -1)
     far_a, far_b = ring(left_a, 1), ring(right_b, -1)
     row_number = home * rows + jnp.arange(rows, dtype=jnp.int32)
     lane = jnp.arange(HD, dtype=jnp.float32)
@@ -307,21 +308,21 @@
         flops // 2,
     )
     halo = shift(hi, 1)
-    upper, q_low = scratch_call(
+    upper, q_low, to_left = scratch_call(
         upper_body,
-        [((2, CH, 512), bf), ((2, CH, 512), bf)],
-        [],
+        [((2, CH, 512), bf), ((2, CH, 512), bf), ((CH, 512), bf)],
+        [block_owner],
         [normed, w_query, cosines, sines, docs, q0, q1, q2, a, b, hi],
         flops,
     )
-    s0, s1, s2, s3, to_left = scratch_call(
-        lower_body, [((CH, 512), bf)] * 5, [block_owner], [halo, a, b, q_low, docs, upper], flops // 2
+    from_right = shift(to_left, -1)
+    s0, s1, s2, s3 = scratch_call(
+        lower_body, [((CH, 512), bf)] * 4, [], [halo, a, b, q_low, docs, upper], flops // 2
     )
     pieces = []
     for by, piece in ((2, s2), (1, s1), (3, s3)):
         pieces.append(ring(piece, by))
     r2, r1, r3 = pieces
-    from_right = shift(to_left, -1)
     cache = jax.ShapeDtypeStruct((rows + 2 * CH, 256), bf)
     key_cache, value_cache = pl.pallas_call(
         cache_body,

time: 70.9 us -> 67.1 us (0.946)
  waiting for transfers between devices: 32.3 us -> 23.5 us
  starting transfers between devices: 17.7 us -> 22.6 us
    ppermute x2, waiting for transfers between devices: 6.44 us -> 0.01 us  [shift(): lax.ppermute(array, 'seq', [(i, i + by) for i in range(n) if 0 <= i + by...]
    ppermute x2, starting transfers between devices: 4.01 us -> 9.07 us  [shift(): lax.ppermute(array, 'seq', [(i, i + by) for i in range(n) if 0 <= i + by...]
    ppermute x9, waiting for transfers between devices: 25.9 us -> 23.5 us  [ring(): return lax.ppermute(array, 'tp', [(i, (i + by) % n) for i in range(n)])]
  transfers between devices with their start and end apart: 11 -> 11, of which waited for: 5 -> 4; matrix products, arithmetic and copies ran while one was open for 2% -> 2% of each run, Pallas kernels for 18% -> 22%
where the time goes in v1:
time: 67.1 us; the launch traced here: 66.9 us
  waiting for transfers between devices  23.5 us (35%)
  starting transfers between devices  22.6 us (34%)
  Pallas kernels  17.4 us (26%)
  local copies, waits for them, and re-layouts  1.41 us (2%)
  other arithmetic  1.01 us (2%)
  between operations  0.95 us (1%)
    ppermute x9, waiting for transfers between devices, ring(): return lax.ppermute(array, 'tp', [(i, (i + by) % n) for i in range(n)])  23.5 us
    ppermute x9, starting transfers between devices, ring(): return lax.ppermute(array, 'tp', [(i, (i + by) % n) for i in range(n)])  13.6 us
    ppermute x2, starting transfers between devices, shift(): lax.ppermute(array, 'seq', [(i, i + by) for i in range(n) if 0 <= i + by...  9.07 us
    pallas_call x3, Pallas kernels, scratch_call(): pl.pallas_call(body, out_shape=[VM(s, d) for s, d in outs], in_specs=[sme...  6.66 us
    pallas_call x3, Pallas kernels, call(): pl.pallas_call(body, out_shape=[VM(s, d) for s, d in outs], in_specs=[sme...  4.88 us
    pallas_call x1, Pallas kernels, mover(): pl.pallas_call(body, out_shape=[VM(s, bf) for s in outs], in_specs=[outsi...  3.51 us
    pallas_call x1, Pallas kernels, layer(): pl.pallas_call(cache_body, out_shape=[cache, cache], in_specs=[smem] + [i...  1.43 us
  transfers between devices with their start and end apart: 11, of which 4 were waited for; matrix products, arithmetic and copies ran while one was open for 2% of the time, Pallas kernels for 22%

profile of v1, /device:TPU:128, one launch (start us, length us, event | category | flops | bytes accessed | tf_op | source)
XLA Modules:
  0.0 66.9 jit_solution(10457247075849640460)
XLA Ops:
  0.6 1.3 %fusion.4 = (bf16[64,4096]{1,0:T(8,128)(2,1)S(1)}, bf16[64,4096]{1,0:T(8,128)(2,1)S(1)}) fusion(bf16[128,4096]{1,0:T(8,128)(2,1)} %param.7), kind=kLoop, calls=%fused_computation.11 | loop fusion | bytes 2097152 | tf_op jit(solution)/shard_map/slice | solution.py:260
  1.9 1.7 %collective-permute-start = (bf16[64,4096]{1,0:T(8,128)(2,1)S(1)}, bf16[64,4096]{1,0:T(8,128)(2,1)S(1)}, u32[]{:S(2)}, u32[]{:S(2)}) collective-permute-start(bf16[64,4096]{1,0:T(8,128)(2,1)S(1)} %get-tuple-element.48.xa), channel_id=1, source_target_pairs={{0,1},{1,2},{2,3},{3,0},{4,5},{5,6},{6,7},{7,4},{8,9},{9,10},{10,1... | collective-permute-start | bytes 1572872 | tf_op jit(solution)/shard_map/ppermute | solution.py:21
  3.6 1.7 %collective-permute-start.2 = (bf16[64,4096]{1,0:T(8,128)(2,1)S(1)}, bf16[64,4096]{1,0:T(8,128)(2,1)S(1)}, u32[]{:S(2)}, u32[]{:S(2)}) collective-permute-start(bf16[64,4096]{1,0:T(8,128)(2,1)S(1)} %get-tuple-element.47.xb), channel_id=1, source_target_pairs={{0,3},{1,0},{2,1},{3,2},{4,7},{5,4},{6,5},{7,6},{8,11},{9,8},{10,9... | collective-permute-start | bytes 1572872 | tf_op jit(solution)/shard_map/ppermute | solution.py:21
  5.2 1.8 %collective-permute-start.5 = (bf16[64,4096]{1,0:T(8,128)(2,1)S(1)}, bf16[64,4096]{1,0:T(8,128)(2,1)S(1)}, u32[]{:S(2)}, u32[]{:S(2)}) collective-permute-start(bf16[64,4096]{1,0:T(8,128)(2,1)S(1)} %get-tuple-element.48.xa), channel_id=1, source_target_pairs={{0,3},{1,0},{2,1},{3,2},{4,7},{5,4},{6,5},{7,6},{8,11},{9,8},{10,9... | collective-permute-start | bytes 1572872 | tf_op jit(solution)/shard_map/ppermute | solution.py:21
  7.0 0.2 collective-permute-start.4
  7.3 0.1 broadcast_in_dim.21.after.docs
  7.4 0.0 copy-start
  7.4 3.5 %shard_map.94 = (bf16[4096,512]{1,0:T(8,128)(2,1)S(1)}, bf16[4096,256]{1,0:T(8,128)(2,1)S(1)}, bf16[4096,256]{1,0:T(8,128)(2,1)S(1)}) custom-call(bf16[4096,512]{1,0:T(8,128)(2,1)} %wq.1, bf16[4096,256]{1,0:T(8,128)(2,1)} %wk.1, bf16[4096,256]{1,0:T(8,128)(2,1)} %wv.1, s32[512,128]{1,0:T(8,128)S(1)} %broadcast_in_dim.21.after.docs), custom_call_target="tpu_custom_call" | custom-call | bytes 16777216 | tf_op jit(solution)/shard_map/pallas_call | solution.py:250
  10.9 7.1 %collective-permute-done.xa = bf16[64,4096]{1,0:T(8,128)(2,1)S(1)} collective-permute-done((bf16[64,4096]{1,0:T(8,128)(2,1)S(1)}, bf16[64,4096]{1,0:T(8,128)(2,1)S(1)}, u32[]{:S(2)}, u32[]{:S(2)}) %collective-permute-start) | collective-permute-done | bytes 524320 | tf_op jit(solution)/shard_map/ppermute | solution.py:21
  18.0 0.4 collective-permute-start.1
  18.4 2.9 %collective-permute-start.3 = (bf16[64,4096]{1,0:T(8,128)(2,1)S(1)}, bf16[64,4096]{1,0:T(8,128)(2,1)S(1)}, u32[]{:S(2)}, u32[]{:S(2)}) collective-permute-start(bf16[64,4096]{1,0:T(8,128)(2,1)S(1)} %collective-permute-done.2.xb), channel_id=1, source_target_pairs={{0,3},{1,0},{2,1},{3,2},{4,7},{5,4},{6,5},{7,6},{8,11},{9,8},{10,9... | collective-permute-start | bytes 1572872 | tf_op jit(solution)/shard_map/ppermute | solution.py:21
  21.2 1.0 %fusion = (f32[512,128]{1,0:T(8,128)S(1)}, f32[512,128]{1,0:T(8,128)S(1)}) fusion(f32[128]{0:T(128)S(1)} %get-tuple-element.53, f32[128]{0:T(128)S(1)} %get-tuple-element.54, f32[512]{0:T(512)S(1)} %get-tuple-element.51), kind=kLoop, calls=%fused_computation.2 | loop fusion | flops 131072 | bytes 527360 | tf_op jit(solution)/shard_map/mul | solution.py:271
  22.2 1.6 %shard_map.95 = (bf16[128,512]{1,0:T(8,128)(2,1)S(1)}, bf16[128,512]{1,0:T(8,128)(2,1)S(1)}) custom-call(bf16[64,4096]{1,0:T(8,128)(2,1)S(1)} %get-tuple-element.48.xa, bf16[64,4096]{1,0:T(8,128)(2,1)S(1)} %get-tuple-element.47.xb, f32[1,4096]{1,0:T(1,128)S(1)} %bitcast.1, bf16[4096,512]{1,0:T(8,128)(2,1)S(1)} %get-tuple-element.27.wq, ...), custom_call_target="tpu_custom_call" | custom-call | flops 1073741824 | bytes 9977856 | tf_op jit(solution)/shard_map/pallas_call | solution.py:42
  23.9 5.7 %collective-permute-done.5.xa = bf16[64,4096]{1,0:T(8,128)(2,1)S(1)} collective-permute-done((bf16[64,4096]{1,0:T(8,128)(2,1)S(1)}, bf16[64,4096]{1,0:T(8,128)(2,1)S(1)}, u32[]{:S(2)}, u32[]{:S(2)}) %collective-permute-start.5) | collective-permute-done | bytes 524320 | tf_op jit(solution)/shard_map/ppermute | solution.py:21
  29.6 1.6 %shard_map.97 = (bf16[128,512]{1,0:T(8,128)(2,1)S(1)}, bf16[128,512]{1,0:T(8,128)(2,1)S(1)}) custom-call(bf16[64,4096]{1,0:T(8,128)(2,1)S(1)} %collective-permute-done.5.xa, bf16[64,4096]{1,0:T(8,128)(2,1)S(1)} %collective-permute-done.2.xb, f32[1,4096]{1,0:T(1,128)S(1)} %bitcast.2, bf16[4096,512]{1,0:T(8,128)(2,1)S(1)} %get-tuple-element.27.wq, ...), custom_call_target="tpu_custom_call" | custom-call | flops 1073741824 | bytes 9977856 | tf_op jit(solution)/shard_map/pallas_call | solution.py:42
  31.2 0.0 copy-start.1
  31.2 0.0 collective-permute-done.4.xb
  31.3 1.6 %shard_map.96 = (bf16[128,512]{1,0:T(8,128)(2,1)S(1)}, bf16[128,512]{1,0:T(8,128)(2,1)S(1)}) custom-call(bf16[64,4096]{1,0:T(8,128)(2,1)S(1)} %collective-permute-done.xa, bf16[64,4096]{1,0:T(8,128)(2,1)S(1)} %collective-permute-done.4.xb, f32[1,4096]{1,0:T(1,128)S(1)} %bitcast.3, bf16[4096,512]{1,0:T(8,128)(2,1)S(1)} %get-tuple-element.27.wq, ...), custom_call_target="tpu_custom_call" | custom-call | flops 1073741824 | bytes 9977856 | tf_op jit(solution)/shard_map/pallas_call | solution.py:42
  32.9 6.5 %collective-permute-done.1.xa = bf16[64,4096]{1,0:T(8,128)(2,1)S(1)} collective-permute-done((bf16[64,4096]{1,0:T(8,128)(2,1)S(1)}, bf16[64,4096]{1,0:T(8,128)(2,1)S(1)}, u32[]{:S(2)}, u32[]{:S(2)}) %collective-permute-start.1) | collective-permute-done | bytes 524320 | tf_op jit(solution)/shard_map/ppermute | solution.py:21
  39.4 0.0 collective-permute-done.3.xb
  39.4 1.7 %shard_map.98 = (bf16[128,4096]{1,0:T(8,128)(2,1)S(1)}, bf16[272,512]{1,0:T(8,128)(2,1)S(1)}, bf16[128,512]{1,0:T(8,128)(2,1)S(1)}, bf16[128,512]{1,0:T(8,128)(2,1)S(1)}) custom-call(s32[16]{0:T(128)S(1)} %copy-done.1, bf16[64,4096]{1,0:T(8,128)(2,1)S(1)} %collective-permute-done.1.xa, bf16[64,4096]{1,0:T(8,128)(2,1)S(1)} %collective-permute-done.3.xb, ...), custom_call_target="tpu_custom_call" | custom-call | flops 536870912 | bytes 1048576 | tf_op jit(solution)/shard_map/pallas_call | solution.py:293
  41.1 2.1 %collective-permute-start.7 = (bf16[272,512]{1,0:T(8,128)(2,1)S(1)}, bf16[272,512]{1,0:T(8,128)(2,1)S(1)}, u32[]{:S(2)}, u32[]{:S(2)}) collective-permute-start(bf16[272,512]{1,0:T(8,128)(2,1)S(1)} %get-tuple-element.37.hi), channel_id=1, source_target_pairs={{0,4},{4,8},{8,12},{12,16},{16,20},{20,24},{24,28},{28,32},{32,36}... | collective-permute-start | bytes 835592 | tf_op jit(solution)/shard_map/ppermute | solution.py:26
  43.2 3.2 %shard_map.99 = (bf16[2,128,512]{2,1,0:T(8,128)(2,1)S(1)}, bf16[2,128,512]{2,1,0:T(8,128)(2,1)S(1)}, bf16[128,512]{1,0:T(8,128)(2,1)S(1)}) custom-call(s32[16]{0:T(128)S(1)} %copy-done.1, bf16[128,4096]{1,0:T(8,128)(2,1)S(1)} %get-tuple-element.31.normed, bf16[4096,512]{1,0:T(8,128)(2,1)S(1)} %get-tuple-element.27.wq, ...), custom_call_target="tpu_custom_call" | custom-call | flops 1073741824 | bytes 1048576 | tf_op jit(solution)/shard_map/pallas_call | solution.py:293
  46.4 7.0 %collective-permute-start.6 = (bf16[128,512]{1,0:T(8,128)(2,1)S(1)}, bf16[128,512]{1,0:T(8,128)(2,1)S(1)}, u32[]{:S(2)}, u32[]{:S(2)}) collective-permute-start(bf16[128,512]{1,0:T(8,128)(2,1)S(1)} %get-tuple-element.38), channel_id=1, source_target_pairs={{4,0},{8,4},{12,8},{16,12},{20,16},{24,20},{28,24},{32,28},{36,32}... | collective-permute-start | bytes 393224 | tf_op jit(solution)/shard_map/ppermute | solution.py:26
  53.4 1.8 %shard_map.100 = (bf16[128,512]{1,0:T(8,128)(2,1)S(1)}, bf16[128,512]{1,0:T(8,128)(2,1)S(1)}, bf16[128,512]{1,0:T(8,128)(2,1)S(1)}, bf16[128,512]{1,0:T(8,128)(2,1)S(1)}) custom-call(bf16[272,512]{1,0:T(8,128)(2,1)S(1)} %collective-permute-done.7.halo, bf16[128,512]{1,0:T(8,128)(2,1)S(1)} %get-tuple-element.35.a, bf16[128,512]{1,0:T(8,128)(2,1)S(1)} %get-tuple-element.36.b, ...), custom_call_target="tpu_custom_call" | custom-call | flops 536870912 | bytes 1048576 | tf_op jit(solution)/shard_map/pallas_call | solution.py:293
  55.2 3.1 %collective-permute-start.10 = (bf16[128,512]{1,0:T(8,128)(2,1)S(1)}, bf16[128,512]{1,0:T(8,128)(2,1)S(1)}, u32[]{:S(2)}, u32[]{:S(2)}) collective-permute-start(bf16[128,512]{1,0:T(8,128)(2,1)S(1)} %get-tuple-element.44), channel_id=1, source_target_pairs={{0,3},{1,0},{2,1},{3,2},{4,7},{5,4},{6,5},{7,6},{8,11},{9,8},{10,9... | collective-permute-start | bytes 393224 | tf_op jit(solution)/shard_map/ppermute | solution.py:21
  58.3 1.9 %collective-permute-start.9 = (bf16[128,512]{1,0:T(8,128)(2,1)S(1)}, bf16[128,512]{1,0:T(8,128)(2,1)S(1)}, u32[]{:S(2)}, u32[]{:S(2)}) collective-permute-start(bf16[128,512]{1,0:T(8,128)(2,1)S(1)} %get-tuple-element.43), channel_id=1, source_target_pairs={{0,2},{1,3},{2,0},{3,1},{4,6},{5,7},{6,4},{7,5},{8,10},{9,11},{10,... | collective-permute-start | bytes 393224 | tf_op jit(solution)/shard_map/ppermute | solution.py:21
  60.2 1.4 %shard_map.101 = (bf16[768,256]{1,0:T(8,128)(2,1)}, bf16[768,256]{1,0:T(8,128)(2,1)}) custom-call(s32[16]{0:T(128)S(1)} %copy-done.1, bf16[272,512]{1,0:T(8,128)(2,1)S(1)} %collective-permute-done.7.halo, bf16[128,512]{1,0:T(8,128)(2,1)S(1)} %get-tuple-element.35.a, bf16[128,512]{1,0:T(8,128)(2,1)S(1)} %get-tuple-element.36.b, ...), custom_call_target="tpu_custom_call" | custom-call | bytes 2097152 | tf_op jit(solution)/shard_map/pallas_call | solution.py:327
  61.6 0.0 collective-permute-done.6.right
  61.7 0.0 collective-permute-done.10.r3
  61.7 4.2 %collective-permute-done.8.r1 = bf16[128,512]{1,0:T(8,128)(2,1)S(1)} collective-permute-done((bf16[128,512]{1,0:T(8,128)(2,1)S(1)}, bf16[128,512]{1,0:T(8,128)(2,1)S(1)}, u32[]{:S(2)}, u32[]{:S(2)}) %collective-permute-start.8) | collective-permute-done | bytes 131104 | tf_op jit(solution)/shard_map/ppermute | solution.py:21
  65.9 0.9 %shard_map.102 = (bf16[128,2048]{1,0:T(8,128)(2,1)}, bf16[768,256]{1,0:T(8,128)(2,1)}, bf16[768,256]{1,0:T(8,128)(2,1)}) custom-call(bf16[128,512]{1,0:T(8,128)(2,1)S(1)} %collective-permute-done.6.right, bf16[128,512]{1,0:T(8,128)(2,1)S(1)} %get-tuple-element.41.s0, ...), custom_call_target="tpu_custom_call", output_to_operand_aliasing={{1}: (5, {}), {2}: (6, {})} | custom-call | bytes 1048576 | tf_op jit(solution)/shard_map/pallas_call | solution.py:336
  (10 shorter events, 0.0 us)
Async XLA Ops:
  0.6 6.6 %copy-start.2 = (s32[512]{0:T(512)S(1)}, s32[512]{0:T(512)}, u32[]{:S(2)}) copy-start(s32[512]{0:T(512)} %param.12) | copy-start | bytes 6148
  1.9 16.1 %collective-permute-start = (bf16[64,4096]{1,0:T(8,128)(2,1)S(1)}, bf16[64,4096]{1,0:T(8,128)(2,1)S(1)}, u32[]{:S(2)}, u32[]{:S(2)}) collective-permute-start(bf16[64,4096]{1,0:T(8,128)(2,1)S(1)} %get-tuple-element.48.xa), channel_id=1, source_target_pairs={{0,1},{1,2},{2,3},{3,0},{4,5},{5,6},{6,7},{7,4},{8,9},{9,10},{10,1... | collective-permute-start | bytes 1572872 | tf_op jit(solution)/shard_map/ppermute | solution.py:21
  3.6 14.8 %collective-permute-start.2 = (bf16[64,4096]{1,0:T(8,128)(2,1)S(1)}, bf16[64,4096]{1,0:T(8,128)(2,1)S(1)}, u32[]{:S(2)}, u32[]{:S(2)}) collective-permute-start(bf16[64,4096]{1,0:T(8,128)(2,1)S(1)} %get-tuple-element.47.xb), channel_id=1, source_target_pairs={{0,3},{1,0},{2,1},{3,2},{4,7},{5,4},{6,5},{7,6},{8,11},{9,8},{10,9... | collective-permute-start | bytes 1572872 | tf_op jit(solution)/shard_map/ppermute | solution.py:21
  5.2 24.4 %collective-permute-start.5 = (bf16[64,4096]{1,0:T(8,128)(2,1)S(1)}, bf16[64,4096]{1,0:T(8,128)(2,1)S(1)}, u32[]{:S(2)}, u32[]{:S(2)}) collective-permute-start(bf16[64,4096]{1,0:T(8,128)(2,1)S(1)} %get-tuple-element.48.xa), channel_id=1, source_target_pairs={{0,3},{1,0},{2,1},{3,2},{4,7},{5,4},{6,5},{7,6},{8,11},{9,8},{10,9... | collective-permute-start | bytes 1572872 | tf_op jit(solution)/shard_map/ppermute | solution.py:21
  7.0 24.2 %collective-permute-start.4 = (bf16[64,4096]{1,0:T(8,128)(2,1)S(1)}, bf16[64,4096]{1,0:T(8,128)(2,1)S(1)}, u32[]{:S(2)}, u32[]{:S(2)}) collective-permute-start(bf16[64,4096]{1,0:T(8,128)(2,1)S(1)} %get-tuple-element.47.xb), channel_id=1, source_target_pairs={{0,1},{1,2},{2,3},{3,0},{4,5},{5,6},{6,7},{7,4},{8,9},{9,10},{10,1... | collective-permute-start | bytes 1572872 | tf_op jit(solution)/shard_map/ppermute | solution.py:21
  7.4 14.8 %copy-start = (f32[4096]{0:T(1024)S(1)}, f32[4096]{0:T(1024)}, u32[]{:S(2)}) copy-start(f32[4096]{0:T(1024)} %param.8) | copy-start | bytes 49156
  18.0 21.4 %collective-permute-start.1 = (bf16[64,4096]{1,0:T(8,128)(2,1)S(1)}, bf16[64,4096]{1,0:T(8,128)(2,1)S(1)}, u32[]{:S(2)}, u32[]{:S(2)}) collective-permute-start(bf16[64,4096]{1,0:T(8,128)(2,1)S(1)} %collective-permute-done.xa), channel_id=1, source_target_pairs={{0,1},{1,2},{2,3},{3,0},{4,5},{5,6},{6,7},{7,4},{8,9},{9,10},{10,1... | collective-permute-start | bytes 1572872 | tf_op jit(solution)/shard_map/ppermute | solution.py:21
  18.4 21.1 %collective-permute-start.3 = (bf16[64,4096]{1,0:T(8,128)(2,1)S(1)}, bf16[64,4096]{1,0:T(8,128)(2,1)S(1)}, u32[]{:S(2)}, u32[]{:S(2)}) collective-permute-start(bf16[64,4096]{1,0:T(8,128)(2,1)S(1)} %collective-permute-done.2.xb), channel_id=1, source_target_pairs={{0,3},{1,0},{2,1},{3,2},{4,7},{5,4},{6,5},{7,6},{8,11},{9,8},{10,9... | collective-permute-start | bytes 1572872 | tf_op jit(solution)/shard_map/ppermute | solution.py:21
  31.2 8.2 %copy-start.1 = (s32[16]{0:T(128)S(1)}, s32[16]{0:T(128)}, u32[]{:S(2)}) copy-start(s32[16]{0:T(128)} %owner.5) | copy-start | bytes 196
  41.1 12.3 %collective-permute-start.7 = (bf16[272,512]{1,0:T(8,128)(2,1)S(1)}, bf16[272,512]{1,0:T(8,128)(2,1)S(1)}, u32[]{:S(2)}, u32[]{:S(2)}) collective-permute-start(bf16[272,512]{1,0:T(8,128)(2,1)S(1)} %get-tuple-element.37.hi), channel_id=1, source_target_pairs={{0,4},{4,8},{8,12},{12,16},{16,20},{20,24},{24,28},{28,32},{32,36}... | collective-permute-start | bytes 835592 | tf_op jit(solution)/shard_map/ppermute | solution.py:26
  46.4 15.2 %collective-permute-start.6 = (bf16[128,512]{1,0:T(8,128)(2,1)S(1)}, bf16[128,512]{1,0:T(8,128)(2,1)S(1)}, u32[]{:S(2)}, u32[]{:S(2)}) collective-permute-start(bf16[128,512]{1,0:T(8,128)(2,1)S(1)} %get-tuple-element.38), channel_id=1, source_target_pairs={{4,0},{8,4},{12,8},{16,12},{20,16},{24,20},{28,24},{32,28},{36,32}... | collective-permute-start | bytes 393224 | tf_op jit(solution)/shard_map/ppermute | solution.py:26
  55.2 6.5 %collective-permute-start.10 = (bf16[128,512]{1,0:T(8,128)(2,1)S(1)}, bf16[128,512]{1,0:T(8,128)(2,1)S(1)}, u32[]{:S(2)}, u32[]{:S(2)}) collective-permute-start(bf16[128,512]{1,0:T(8,128)(2,1)S(1)} %get-tuple-element.44), channel_id=1, source_target_pairs={{0,3},{1,0},{2,1},{3,2},{4,7},{5,4},{6,5},{7,6},{8,11},{9,8},{10,9... | collective-permute-start | bytes 393224 | tf_op jit(solution)/shard_map/ppermute | solution.py:21
  58.3 7.6 %collective-permute-start.8 = (bf16[128,512]{1,0:T(8,128)(2,1)S(1)}, bf16[128,512]{1,0:T(8,128)(2,1)S(1)}, u32[]{:S(2)}, u32[]{:S(2)}) collective-permute-start(bf16[128,512]{1,0:T(8,128)(2,1)S(1)} %get-tuple-element.42), channel_id=1, source_target_pairs={{0,1},{1,2},{2,3},{3,0},{4,5},{5,6},{6,7},{7,4},{8,9},{9,10},{10,1... | collective-permute-start | bytes 393224 | tf_op jit(solution)/shard_map/ppermute | solution.py:21
  58.3 7.6 %collective-permute-start.9 = (bf16[128,512]{1,0:T(8,128)(2,1)S(1)}, bf16[128,512]{1,0:T(8,128)(2,1)S(1)}, u32[]{:S(2)}, u32[]{:S(2)}) collective-permute-start(bf16[128,512]{1,0:T(8,128)(2,1)S(1)} %get-tuple-element.43), channel_id=1, source_target_pairs={{0,2},{1,3},{2,0},{3,1},{4,6},{5,7},{6,4},{7,5},{8,10},{9,11},{10,... | collective-permute-start | bytes 393224 | tf_op jit(solution)/shard_map/ppermute | solution.py:21

commit v2 on v1

v2 whole, which is shorter than its diff:
```python
import jax
import jax.numpy as jnp
from jax import lax
from jax.experimental import pallas as pl
from jax.experimental.pallas import tpu as pltpu
from jax.sharding import PartitionSpec as P


HD = 128
EPS = 1e-05
ROPE_BASE = 500000.0
CH = 128
VM = pltpu.MemorySpace.VMEM
HB = pltpu.MemorySpace.HBM


def ring(array, by):
    n = lax.axis_size("tp")
    return lax.ppermute(array, "tp", [(i, (i + by) % n) for i in range(n)])


def across(array, moves):
    homes, n = lax.axis_size("seq"), lax.axis_size("tp")
    pairs = [(h * n + t, (h + by) * n + t) for h in range(homes) for t, by in moves.items() if 0 <= h + by < homes]
    return lax.ppermute(array, ("seq", "tp"), pairs)


def spots():
    me, home = lax.axis_index("tp"), lax.axis_index("seq")
    return [lax.rem(me + k, 4) for k in (0, 3, 1, 2)] + [home]


def vmem(x):
    return pltpu.with_memory_space_constraint(x, VM)


def call(body, outs, arrays, flops=0, owner=None, alias=None, scratch=()):
    smem = pl.BlockSpec(memory_space=pltpu.SMEM)
    inside = pl.BlockSpec(memory_space=VM)
    lead = [] if owner is None else [owner]
    moved = sum(x.size * x.dtype.itemsize for x in arrays)
    return pl.pallas_call(
        body,
        out_shape=[o if isinstance(o, jax.ShapeDtypeStruct) else VM(o, jnp.bfloat16) for o in outs],
        in_specs=[smem] * len(lead) + [inside] * len(arrays),
        out_specs=[
            pl.BlockSpec(memory_space=HB) if isinstance(o, jax.ShapeDtypeStruct) else inside for o in outs
        ],
        scratch_shapes=list(scratch),
        input_output_aliases={} if alias is None else {len(lead) + alias: 0},
        compiler_params=pltpu.CompilerParams(vmem_limit_bytes=12 << 20),
        cost_estimate=pl.CostEstimate(flops=flops, bytes_accessed=moved, transcendentals=0),
    )(*lead, *[vmem(x) for x in arrays])


def normalize(x, gain):
    wide = x.astype(jnp.float32)
    inverse = lax.rsqrt(jnp.mean(wide * wide, axis=1, keepdims=True) + EPS)
    return (wide * inverse * gain).astype(jnp.bfloat16)


def rotate(x, cosine, sine):
    heads = x.shape[1] // HD
    parts = []
    for i in range(heads):
        one = x[:, i * HD : (i + 1) * HD]
        parts.append((one * cosine + pltpu.roll(one, HD // 2, 1) * sine).astype(jnp.bfloat16))
    return parts


def dot(a, b):
    return jnp.dot(a, b, preferred_element_type=jnp.float32)


def project_kv(normed, wk, wv, cosine, sine):
    keys = rotate(dot(normed, wk[...]), cosine, sine)
    values = dot(normed, wv[...]).astype(jnp.bfloat16)
    return keys, values


def project_q(normed, wq, cosine, sine):
    parts = []
    for i in range(wq.shape[1] // 256):
        parts += rotate(dot(normed, wq[:, i * 256 : (i + 1) * 256]), cosine, sine)
    return parts


def run(copies):
    for copy in copies:
        copy.start()
    for copy in copies:
        copy.wait()


def weights_body(wq, wk, wv, after, wq_out, wk_out, wv_out, sems):
    run([pltpu.make_async_copy(w, out, sems.at[i]) for i, (w, out) in enumerate(((wq, wq_out), (wk, wk_out), (wv, wv_out)))])


def chunk_rows(at):
    return pl.ds(pl.multiple_of(at * CH, CH), CH)


def normalize_all(pieces, gain):
    return jnp.concatenate([normalize(piece[...], gain[...]) for piece in pieces], axis=0)


def put(ref, index, rows, parts):
    for i, part in enumerate(parts):
        ref[index, :, i * HD : (i + 1) * HD] = part[rows]


def kv_parts(normed, wk, wv, cosine, sine):
    keys, values = project_kv(normed, wk, wv, cosine, sine)
    return [*keys, values[:, :HD], values[:, HD:]]


def own_body(xa, xb, gain, wq, wk, wv, cosines, sines, ext, q_out):
    own = spots()[0]
    rows = chunk_rows(own)
    normed = normalize_all((xa, xb), gain)
    put(ext, 2 + own, slice(None), kv_parts(normed, wk, wv, cosines[rows], sines[rows]))
    for i, part in enumerate(project_q(normed, wq, cosines[rows], sines[rows])):
        q_out[:, i * HD : (i + 1) * HD] = part


def owned_part(part, live):
    return jnp.where(live, part, jnp.zeros_like(part))


def sides_body(owner, ext_in, ra, rb, la, lb, gain, wk, wv, cosines, sines, ext, normed_out, hi_out, left_out):
    _, left, right, _, home = spots()
    normed = normalize_all((ra, rb, la, lb), gain)
    normed_out[...] = normed
    rows = [chunk_rows(right), chunk_rows(left)]
    cosine = jnp.concatenate([cosines[r] for r in rows], axis=0)
    sine = jnp.concatenate([sines[r] for r in rows], axis=0)
    parts = kv_parts(normed, wk, wv, cosine, sine)
    put(ext, 2 + right, slice(0, CH), parts)
    put(ext, 2 + left, slice(CH, 2 * CH), parts)
    hi_out[0:CH] = ext[4]
    hi_out[CH : 2 * CH] = ext[5]
    count = jnp.int32(0)
    for j in range(4):
        count += (owner[12 + j] == home + 1).astype(jnp.int32)
    hi_out[2 * CH : 2 * CH + 16] = jnp.full((16, 512), count.astype(jnp.float32), jnp.float32).astype(jnp.bfloat16)
    for j in range(4):
        left_out[j * 32 : (j + 1) * 32] = owned_part(ext[2, j * 32 : (j + 1) * 32], owner[j] == home - 1)


def sides_q_body(normed, wq, cosines, sines, right_out, left_out):
    _, left, right, _, _ = spots()
    rows = [chunk_rows(right), chunk_rows(left)]
    cosine = jnp.concatenate([cosines[r] for r in rows], axis=0)
    sine = jnp.concatenate([sines[r] for r in rows], axis=0)
    for i, part in enumerate(project_q(normed[...], wq, cosine, sine)):
        right_out[:, i * HD : (i + 1) * HD] = part[:CH]
        left_out[:, i * HD : (i + 1) * HD] = part[CH:]


def attend(tile, q, ext, docs):
    window = 3 * CH
    doc = docs[chunk_rows(tile), 0:1]
    key_row = lax.broadcasted_iota(jnp.int32, (CH, window), 1) + (tile - 2) * CH
    row = lax.broadcasted_iota(jnp.int32, (CH, window), 0) + tile * CH
    allowed = (key_row >= doc) & (key_row <= row)
    allowed = jnp.concatenate([allowed, allowed], axis=0)
    near = ext[pl.ds(tile, 3)].reshape(window, 512)
    outs = []
    for g in range(2):
        pair = jnp.concatenate(q[2 * g : 2 * g + 2], axis=0)
        keys, values = near[:, g * HD : (g + 1) * HD], near[:, (2 + g) * HD : (3 + g) * HD]
        scores = lax.dot_general(pair, keys, (((1,), (1,)), ((), ())), preferred_element_type=jnp.float32) * HD ** (-0.5)
        scores = jnp.where(allowed, scores, -jnp.inf)
        highest = jnp.max(scores, axis=1, keepdims=True)
        weights = jnp.exp(scores - highest)
        weights = (weights * (1.0 / jnp.sum(weights, axis=1, keepdims=True))).astype(jnp.bfloat16)
        blended = dot(weights, values).astype(jnp.bfloat16)
        outs += [blended[:CH], blended[CH:]]
    return outs


def heads(q):
    return [q[:, i * HD : (i + 1) * HD] for i in range(4)]


def emit(out, parts):
    for i, part in enumerate(parts):
        out[:, i * HD : (i + 1) * HD] = part


def first_body(ext_in, halo, q, docs, ext, out):
    _, _, right, _, _ = spots()
    ext[0] = halo[0:CH]
    ext[1] = halo[CH : 2 * CH]
    emit(out, attend(right, heads(q), ext, docs))


def last_body(owner, ext_in, xa, xb, gain, wk, wv, cosines, sines, ext, normed_out, late_out):
    _, _, _, far, home = spots()
    rows = chunk_rows(far)
    normed = normalize_all((xa, xb), gain)
    normed_out[...] = normed
    parts = kv_parts(normed, wk, wv, cosines[rows], sines[rows])
    put(ext, 2 + far, slice(None), parts)
    for j in range(4):
        live = (far > 0) | (owner[j] == home - 1)
        for i, part in enumerate(parts):
            late_out[j * 32 : (j + 1) * 32, i * HD : (i + 1) * HD] = owned_part(part[j * 32 : (j + 1) * 32], live)


def far_body(ext_in, normed, wq, cosines, sines, docs, ext, out):
    far = spots()[3]
    rows = chunk_rows(far)
    q = project_q(normed[...], wq, cosines[rows], sines[rows])
    emit(out, attend(far, q, ext, docs))


def left_body(ext_in, late, q, docs, ext, out):
    own, left, _, _, _ = spots()

    @pl.when(own < 2)
    def _():
        ext[own] = late[...]

    emit(out, attend(left, heads(q), ext, docs))


def own_tile_body(owner, ext, late, halo, from_right, q, docs, out, key_out, value_out, keys, values, sems):
    own, _, _, _, home = spots()

    def put_cache(row, part):
        keys[row : row + part.shape[0]] = part[:, 0:256]
        values[row : row + part.shape[0]] = part[:, 256:512]

    count = halo[2 * CH : 2 * CH + 1, :].astype(jnp.float32)
    for j in range(4):
        part = ext[1, j * 32 : (j + 1) * 32]
        put_cache(j * 32, jnp.where(count > 3.5 - j, part.astype(jnp.float32), 0.0).astype(jnp.bfloat16))
    for j in range(16):
        part = ext[2 + j // 4, (j % 4) * 32 : (j % 4 + 1) * 32]
        put_cache(CH + j * 32, owned_part(part, owner[j] == home))

    @pl.when(own == 2)
    def _():
        put_cache(5 * CH, late[...])

    @pl.when(own != 2)
    def _():
        put_cache(5 * CH, from_right[...])

    copies = [
        pltpu.make_async_copy(keys, key_out, sems.at[0]),
        pltpu.make_async_copy(values, value_out, sems.at[1]),
    ]
    for copy in copies:
        copy.start()
    emit(out, attend(own, heads(q), ext, docs))
    for copy in copies:
        copy.wait()


def join_body(s0, r1, r2, r3, out, sems):
    own, left, right, far, _ = spots()
    copies = []
    for i, (piece, at) in enumerate(((s0, own), (r1, left), (r2, far), (r3, right))):
        columns = pl.ds(pl.multiple_of(at * 512, 512), 512)
        copies.append(pltpu.make_async_copy(piece, out.at[:, columns], sems.at[i]))
    run(copies)


def layer(hidden, norm_gain, w_query, w_key, w_value, doc_start, block_owner):
    home = lax.axis_index("seq")
    rows = doc_start.shape[0]
    bf = jnp.bfloat16
    inside = pl.BlockSpec(memory_space=VM)
    outside = pl.BlockSpec(memory_space=pltpu.MemorySpace.HBM)
    wide = hidden.shape[1]

    def mover(body, outs, arrays, size):
        return pl.pallas_call(
            body,
            out_shape=[VM(s, bf) for s in outs],
            in_specs=[outside if x.size > CH * wide // 2 else pl.BlockSpec(memory_space=pl.ANY) for x in arrays],
            out_specs=[inside] * len(outs),
            scratch_shapes=[pltpu.SemaphoreType.DMA((len(outs),))],
            compiler_params=pltpu.CompilerParams(vmem_limit_bytes=2 << 20),
            cost_estimate=pl.CostEstimate(flops=0, bytes_accessed=size, transcendentals=0),
        )(*[pltpu.with_memory_space_constraint(x, HB) if x.size > CH * wide // 2 else x for x in arrays])

    own_a, own_b = hidden[: CH // 2], hidden[CH // 2 :]
    left_a = ring(own_a, 1)
    right_b = ring(own_b, -1)
    left_b = ring(own_b, 1)
    right_a = ring(own_a, -1)
    far_a, far_b = ring(left_a, 1), ring(right_b, -1)
    row_number = home * rows + jnp.arange(rows, dtype=jnp.int32)
    lane = jnp.arange(HD, dtype=jnp.float32)
    lane_half = jnp.where(lane < HD // 2, lane, lane - HD // 2)
    frequency = jnp.power(ROPE_BASE, -lane_half * (2.0 / HD))
    angles = (row_number - doc_start).astype(jnp.float32)[:, None] * frequency[None, :]
    cosines, sines = jnp.cos(angles), jnp.where(lane < HD // 2, -1.0, 1.0)[None, :] * jnp.sin(angles)
    docs = jnp.broadcast_to((doc_start - home * rows)[:, None], (rows, HD))

    w_query, w_key, w_value = mover(
        weights_body, [w.shape for w in (w_query, w_key, w_value)], [w_query, w_key, w_value, docs], 16 << 20
    )
    gain = norm_gain[None, :]
    flops = 2 * CH * wide * 1024
    scores = 8 * 2 * CH * 3 * CH * HD
    slots = (6, CH, 512)
    piece = (CH, 512)
    ext, q_own = call(own_body, [slots, piece], [own_a, own_b, gain, w_query, w_key, w_value, cosines, sines], flops)
    ext, normed, hi, to_left = call(
        sides_body,
        [slots, (2 * CH, wide), (2 * CH + 16, 512), piece],
        [ext, right_a, right_b, left_a, left_b, gain, w_key, w_value, cosines, sines],
        flops,
        owner=block_owner,
        alias=0,
    )
    halo = across(hi, {t: 1 for t in range(4)})
    from_right = across(to_left, {t: -1 for t in (0, 1, 3)})
    q_right, q_left = call(sides_q_body, [piece, piece], [normed, w_query, cosines, sines], flops)
    ext, s1 = call(first_body, [slots, piece], [ext, halo, q_right, docs], scores, alias=0)
    r1 = ring(s1, 1)
    ext, normed, far = call(
        last_body,
        [slots, (CH, wide), piece],
        [ext, far_a, far_b, gain, w_key, w_value, cosines, sines],
        flops // 2,
        owner=block_owner,
        alias=0,
    )
    late = across(far, {0: 1, 1: 1, 2: -1})
    ext, s2 = call(far_body, [slots, piece], [ext, normed, w_query, cosines, sines, docs], flops, alias=0)
    r2 = ring(s2, 2)
    ext, s3 = call(left_body, [slots, piece], [ext, late, q_left, docs], scores, alias=0)
    r3 = ring(s3, 3)
    cache = jax.ShapeDtypeStruct((rows + 2 * CH, 256), bf)
    s0, key_cache, value_cache = call(
        own_tile_body,
        [piece, cache, cache],
        [ext, late, halo, from_right, q_own, docs],
        scores,
        owner=block_owner,
        scratch=[VM((rows + 2 * CH, 256), bf)] * 2 + [pltpu.SemaphoreType.DMA((2,))],
    )
    (context,) = call(
        join_body,
        [jax.ShapeDtypeStruct((CH, 2048), bf)],
        [s0, r1, r2, r3],
        scratch=[pltpu.SemaphoreType.DMA((4,))],
    )
    return (context, key_cache, value_cache)


def solution(mesh):
    return jax.shard_map(
        layer,
        mesh=mesh,
        in_specs=(
            P(("seq", "tp"), None),
            P(),
            P(None, "tp"),
            P(None, "tp"),
            P(None, "tp"),
            P("seq"),
            P("seq"),
        ),
        out_specs=(P(("seq", "tp"), None), P("seq", "tp"), P("seq", "tp")),
        check_vma=False,
    )
```

time: 67.1 us -> 66.6 us (level)
  starting transfers between devices: 22.6 us -> 24 us
  waiting for transfers between devices: 23.5 us -> 22.1 us
  Pallas kernels: 17.4 us -> 16.7 us
    ppermute x9, waiting for transfers between devices: 23.5 us -> 14.3 us  [ring(): return lax.ppermute(array, 'tp', [(i, (i + by) % n) for i in range(n)])]
    ppermute x2 -> x3, waiting for transfers between devices: 0.01 us -> 7.84 us  [across(): return lax.ppermute(array, ('seq', 'tp'), pairs)]
    ppermute x2 -> x3, starting transfers between devices: 9.07 us -> 10.8 us  [across(): return lax.ppermute(array, ('seq', 'tp'), pairs)]
    pallas_call x8 -> x9, Pallas kernels: 13.9 us -> 13.2 us  [call(): pl.pallas_call(body, out_shape=[o if isinstance(o, jax.ShapeDtypeStruct)...]
  transfers between devices with their start and end apart: 11 -> 12, of which waited for: 4 -> 5; matrix products, arithmetic and copies ran while one was open for 2% -> 2% of each run, Pallas kernels for 22% -> 22%
where the time goes in v2:
time: 66.6 us; the launch traced here: 66.3 us
  starting transfers between devices  24 us (36%)
  waiting for transfers between devices  22.1 us (33%)
  Pallas kernels  16.7 us (25%)
  local copies, waits for them, and re-layouts  1.41 us (2%)
  other arithmetic  1.01 us (2%)
  between operations  0.99 us (1%)
    ppermute x9, waiting for transfers between devices, ring(): return lax.ppermute(array, 'tp', [(i, (i + by) % n) for i in range(n)])  14.3 us
    pallas_call x9, Pallas kernels, call(): pl.pallas_call(body, out_shape=[o if isinstance(o, jax.ShapeDtypeStruct)...  13.2 us
    ppermute x9, starting transfers between devices, ring(): return lax.ppermute(array, 'tp', [(i, (i + by) % n) for i in range(n)])  13.2 us
    ppermute x3, starting transfers between devices, across(): return lax.ppermute(array, ('seq', 'tp'), pairs)  10.8 us
    ppermute x3, waiting for transfers between devices, across(): return lax.ppermute(array, ('seq', 'tp'), pairs)  7.84 us
    pallas_call x1, Pallas kernels, mover(): pl.pallas_call(body, out_shape=[VM(s, bf) for s in outs], in_specs=[outsi...  3.51 us
  transfers between devices with their start and end apart: 12, of which 5 were waited for; matrix products, arithmetic and copies ran while one was open for 2% of the time, Pallas kernels for 22%

profile of v2, /device:TPU:128, one launch (start us, length us, event | category | flops | bytes accessed | tf_op | source)
XLA Modules:
  0.0 66.3 jit_solution(1208628137833315279)
XLA Ops:
  0.6 1.3 %fusion.4 = (bf16[64,4096]{1,0:T(8,128)(2,1)S(1)}, bf16[64,4096]{1,0:T(8,128)(2,1)S(1)}) fusion(bf16[128,4096]{1,0:T(8,128)(2,1)} %param.7), kind=kLoop, calls=%fused_computation.11 | loop fusion | bytes 2097152 | tf_op jit(solution)/shard_map/slice | solution.py:290
  1.9 1.7 %collective-permute-start.2 = (bf16[64,4096]{1,0:T(8,128)(2,1)S(1)}, bf16[64,4096]{1,0:T(8,128)(2,1)S(1)}, u32[]{:S(2)}, u32[]{:S(2)}) collective-permute-start(bf16[64,4096]{1,0:T(8,128)(2,1)S(1)} %get-tuple-element.50.xa), channel_id=1, source_target_pairs={{0,1},{1,2},{2,3},{3,0},{4,5},{5,6},{6,7},{7,4},{8,9},{9,10},{10,1... | collective-permute-start | bytes 1572872 | tf_op jit(solution)/shard_map/ppermute | solution.py:19
  3.6 1.7 %collective-permute-start.1 = (bf16[64,4096]{1,0:T(8,128)(2,1)S(1)}, bf16[64,4096]{1,0:T(8,128)(2,1)S(1)}, u32[]{:S(2)}, u32[]{:S(2)}) collective-permute-start(bf16[64,4096]{1,0:T(8,128)(2,1)S(1)} %get-tuple-element.49.xb), channel_id=1, source_target_pairs={{0,3},{1,0},{2,1},{3,2},{4,7},{5,4},{6,5},{7,6},{8,11},{9,8},{10,9... | collective-permute-start | bytes 1572872 | tf_op jit(solution)/shard_map/ppermute | solution.py:19
  5.2 1.8 %collective-permute-start = (bf16[64,4096]{1,0:T(8,128)(2,1)S(1)}, bf16[64,4096]{1,0:T(8,128)(2,1)S(1)}, u32[]{:S(2)}, u32[]{:S(2)}) collective-permute-start(bf16[64,4096]{1,0:T(8,128)(2,1)S(1)} %get-tuple-element.50.xa), channel_id=1, source_target_pairs={{0,3},{1,0},{2,1},{3,2},{4,7},{5,4},{6,5},{7,6},{8,11},{9,8},{10,9... | collective-permute-start | bytes 1572872 | tf_op jit(solution)/shard_map/ppermute | solution.py:19
  7.0 0.2 collective-permute-start.3
  7.3 10.7 %collective-permute-done.2.la = bf16[64,4096]{1,0:T(8,128)(2,1)S(1)} collective-permute-done((bf16[64,4096]{1,0:T(8,128)(2,1)S(1)}, bf16[64,4096]{1,0:T(8,128)(2,1)S(1)}, u32[]{:S(2)}, u32[]{:S(2)}) %collective-permute-start.2) | collective-permute-done | bytes 524320 | tf_op jit(solution)/shard_map/ppermute | solution.py:19
  18.0 0.4 collective-permute-start.5
  18.4 2.9 %collective-permute-start.6 = (bf16[64,4096]{1,0:T(8,128)(2,1)S(1)}, bf16[64,4096]{1,0:T(8,128)(2,1)S(1)}, u32[]{:S(2)}, u32[]{:S(2)}) collective-permute-start(bf16[64,4096]{1,0:T(8,128)(2,1)S(1)} %collective-permute-done.1.rb), channel_id=1, source_target_pairs={{0,3},{1,0},{2,1},{3,2},{4,7},{5,4},{6,5},{7,6},{8,11},{9,8},{10,9... | collective-permute-start | bytes 1572872 | tf_op jit(solution)/shard_map/ppermute | solution.py:19
  21.2 1.0 %fusion = (f32[512,128]{1,0:T(8,128)S(1)}, f32[512,128]{1,0:T(8,128)S(1)}) fusion(f32[128]{0:T(128)S(1)} %get-tuple-element.55, f32[128]{0:T(128)S(1)} %get-tuple-element.56, f32[512]{0:T(512)S(1)} %get-tuple-element.53), kind=kLoop, calls=%fused_computation.2 | loop fusion | flops 131072 | bytes 527360 | tf_op jit(solution)/shard_map/mul | solution.py:301
  22.2 0.1 broadcast_in_dim.21.after.docs
  22.4 0.0 copy-start
  22.4 3.5 %shard_map.94 = (bf16[4096,512]{1,0:T(8,128)(2,1)S(1)}, bf16[4096,256]{1,0:T(8,128)(2,1)S(1)}, bf16[4096,256]{1,0:T(8,128)(2,1)S(1)}) custom-call(bf16[4096,512]{1,0:T(8,128)(2,1)} %wq.1, bf16[4096,256]{1,0:T(8,128)(2,1)} %wk.1, bf16[4096,256]{1,0:T(8,128)(2,1)} %wv.1, s32[512,128]{1,0:T(8,128)S(1)} %broadcast_in_dim.21.after.docs), custom_call_target="tpu_custom_call" | custom-call | bytes 16777216 | tf_op jit(solution)/shard_map/pallas_call | solution.py:280
  25.9 0.0 copy-start.1
  25.9 1.6 %shard_map.95 = (bf16[6,128,512]{2,1,0:T(8,128)(2,1)S(1)}, bf16[128,512]{1,0:T(8,128)(2,1)S(1)}) custom-call(bf16[64,4096]{1,0:T(8,128)(2,1)S(1)} %get-tuple-element.50.xa, bf16[64,4096]{1,0:T(8,128)(2,1)S(1)} %get-tuple-element.49.xb, f32[1,4096]{1,0:T(1,128)S(1)} %bitcast.1, bf16[4096,512]{1,0:T(8,128)(2,1)S(1)} %get-tuple-element.26.wq, ...), custom_call_target="tpu_custom_call" | custom-call | flops 1073741824 | bytes 9977856 | tf_op jit(solution)/shard_map/pallas_call | solution.py:42
  27.6 2.0 %collective-permute-done.ra = bf16[64,4096]{1,0:T(8,128)(2,1)S(1)} collective-permute-done((bf16[64,4096]{1,0:T(8,128)(2,1)S(1)}, bf16[64,4096]{1,0:T(8,128)(2,1)S(1)}, u32[]{:S(2)}, u32[]{:S(2)}) %collective-permute-start) | collective-permute-done | bytes 524320 | tf_op jit(solution)/shard_map/ppermute | solution.py:19
  29.6 2.5 %shard_map.96 = (bf16[6,128,512]{2,1,0:T(8,128)(2,1)S(1)}, bf16[256,4096]{1,0:T(8,128)(2,1)S(1)}, bf16[272,512]{1,0:T(8,128)(2,1)S(1)}, bf16[128,512]{1,0:T(8,128)(2,1)S(1)}) custom-call(s32[16]{0:T(128)S(1)} %copy-done.1, bf16[6,128,512]{2,1,0:T(8,128)(2,1)S(1)} %get-tuple-element.29.ext_in, ...), custom_call_target="tpu_custom_call", output_to_operand_aliasing={{0}: (1, {})} | custom-call | flops 1073741824 | bytes 7618560 | tf_op jit(solution)/shard_map/pallas_call | solution.py:42
  32.1 1.9 %collective-permute-start.4 = (bf16[272,512]{1,0:T(8,128)(2,1)S(1)}, bf16[272,512]{1,0:T(8,128)(2,1)S(1)}, u32[]{:S(2)}, u32[]{:S(2)}) collective-permute-start(bf16[272,512]{1,0:T(8,128)(2,1)S(1)} %get-tuple-element.31), channel_id=1, source_target_pairs={{0,4},{1,5},{2,6},{3,7},{4,8},{5,9},{6,10},{7,11},{8,12},{9,13},{1... | collective-permute-start | bytes 835592 | tf_op jit(solution)/shard_map/ppermute | solution.py:25
  34.0 1.4 %shard_map.97 = (bf16[128,512]{1,0:T(8,128)(2,1)S(1)}, bf16[128,512]{1,0:T(8,128)(2,1)S(1)}) custom-call(bf16[256,4096]{1,0:T(8,128)(2,1)S(1)} %get-tuple-element.32.normed, bf16[4096,512]{1,0:T(8,128)(2,1)S(1)} %get-tuple-element.26.wq, f32[512,128]{1,0:T(8,128)S(1)} %get-tuple-element.52.cosines, f32[512,128]{1,0:T(8,128)S(1)} %get-tuple-element.51.sines), custom_call_target="tpu_custom_call" | custom-call | flops 1073741824 | bytes 6815744 | tf_op jit(solution)/shard_map/pallas_call | solution.py:42
  35.4 7.8 %collective-permute-done.4.halo = bf16[272,512]{1,0:T(8,128)(2,1)S(1)} collective-permute-done((bf16[272,512]{1,0:T(8,128)(2,1)S(1)}, bf16[272,512]{1,0:T(8,128)(2,1)S(1)}, u32[]{:S(2)}, u32[]{:S(2)}) %collective-permute-start.4) | collective-permute-done | bytes 278560 | tf_op jit(solution)/shard_map/ppermute | solution.py:25
  43.3 1.0 %shard_map.98 = (bf16[6,128,512]{2,1,0:T(8,128)(2,1)S(1)}, bf16[128,512]{1,0:T(8,128)(2,1)S(1)}) custom-call(bf16[6,128,512]{2,1,0:T(8,128)(2,1)S(1)} %get-tuple-element.30.ext_in, bf16[272,512]{1,0:T(8,128)(2,1)S(1)} %collective-permute-done.4.halo, bf16[128,512]{1,0:T(8,128)(2,1)S(1)} %get-tuple-element.33.q, ...), custom_call_target="tpu_custom_call", output_to_operand_aliasing={{0}: (0, {})} | custom-call | flops 100663296 | bytes 1458176 | tf_op jit(solution)/shard_map/pallas_call | solution.py:42
  44.3 1.6 %shard_map.99 = (bf16[6,128,512]{2,1,0:T(8,128)(2,1)S(1)}, bf16[128,4096]{1,0:T(8,128)(2,1)S(1)}, bf16[128,512]{1,0:T(8,128)(2,1)S(1)}) custom-call(s32[16]{0:T(128)S(1)} %copy-done.1, bf16[6,128,512]{2,1,0:T(8,128)(2,1)S(1)} %get-tuple-element.34.ext_in, bf16[64,4096]{1,0:T(8,128)(2,1)S(1)} %collective-permute-done.5.xa, ...), custom_call_target="tpu_custom_call", output_to_operand_aliasing={{0}: (1, {})} | custom-call | flops 536870912 | bytes 6569984 | tf_op jit(solution)/shard_map/pallas_call | solution.py:42
  45.9 1.9 %collective-permute-start.7 = (bf16[128,512]{1,0:T(8,128)(2,1)S(1)}, bf16[128,512]{1,0:T(8,128)(2,1)S(1)}, u32[]{:S(2)}, u32[]{:S(2)}) collective-permute-start(bf16[128,512]{1,0:T(8,128)(2,1)S(1)} %get-tuple-element.38), channel_id=1, source_target_pairs={{0,4},{1,5},{4,8},{5,9},{6,2},{8,12},{9,13},{10,6},{12,16},{13,17}... | collective-permute-start | bytes 393224 | tf_op jit(solution)/shard_map/ppermute | solution.py:25
  47.8 7.0 %collective-permute-start.8 = (bf16[128,512]{1,0:T(8,128)(2,1)S(1)}, bf16[128,512]{1,0:T(8,128)(2,1)S(1)}, u32[]{:S(2)}, u32[]{:S(2)}) collective-permute-start(bf16[128,512]{1,0:T(8,128)(2,1)S(1)} %get-tuple-element.41), channel_id=1, source_target_pairs={{4,0},{5,1},{7,3},{8,4},{9,5},{11,7},{12,8},{13,9},{15,11},{16,12}... | collective-permute-start | bytes 393224 | tf_op jit(solution)/shard_map/ppermute | solution.py:25
  54.8 1.8 %collective-permute-start.9 = (bf16[128,512]{1,0:T(8,128)(2,1)S(1)}, bf16[128,512]{1,0:T(8,128)(2,1)S(1)}, u32[]{:S(2)}, u32[]{:S(2)}) collective-permute-start(bf16[128,512]{1,0:T(8,128)(2,1)S(1)} %get-tuple-element.44), channel_id=1, source_target_pairs={{0,1},{1,2},{2,3},{3,0},{4,5},{5,6},{6,7},{7,4},{8,9},{9,10},{10,1... | collective-permute-start | bytes 393224 | tf_op jit(solution)/shard_map/ppermute | solution.py:19
  56.6 1.7 %shard_map.100 = (bf16[6,128,512]{2,1,0:T(8,128)(2,1)S(1)}, bf16[128,512]{1,0:T(8,128)(2,1)S(1)}) custom-call(bf16[6,128,512]{2,1,0:T(8,128)(2,1)S(1)} %get-tuple-element.35.ext_in, bf16[128,4096]{1,0:T(8,128)(2,1)S(1)} %get-tuple-element.36.normed, bf16[4096,512]{1,0:T(8,128)(2,1)S(1)} %get-tuple-element.26.wq, ...), custom_call_target="tpu_custom_call", output_to_operand_aliasing={{0}: (0, {})} | custom-call | flops 1073741824 | bytes 6815744 | tf_op jit(solution)/shard_map/pallas_call | solution.py:42
  58.3 0.1 collective-permute-start.10
  58.5 1.0 %shard_map.101 = (bf16[6,128,512]{2,1,0:T(8,128)(2,1)S(1)}, bf16[128,512]{1,0:T(8,128)(2,1)S(1)}) custom-call(bf16[6,128,512]{2,1,0:T(8,128)(2,1)S(1)} %get-tuple-element.37.ext_in, bf16[128,512]{1,0:T(8,128)(2,1)S(1)} %collective-permute-done.7.late, bf16[128,512]{1,0:T(8,128)(2,1)S(1)} %get-tuple-element.39.q, ...), custom_call_target="tpu_custom_call", output_to_operand_aliasing={{0}: (0, {})} | custom-call | flops 100663296 | bytes 1310720 | tf_op jit(solution)/shard_map/pallas_call | solution.py:42
  59.5 2.7 %collective-permute-start.11 = (bf16[128,512]{1,0:T(8,128)(2,1)S(1)}, bf16[128,512]{1,0:T(8,128)(2,1)S(1)}, u32[]{:S(2)}, u32[]{:S(2)}) collective-permute-start(bf16[128,512]{1,0:T(8,128)(2,1)S(1)} %get-tuple-element.46), channel_id=1, source_target_pairs={{0,3},{1,0},{2,1},{3,2},{4,7},{5,4},{6,5},{7,6},{8,11},{9,8},{10,9... | collective-permute-start | bytes 393224 | tf_op jit(solution)/shard_map/ppermute | solution.py:19
  62.2 1.6 %shard_map.102 = (bf16[128,512]{1,0:T(8,128)(2,1)S(1)}, bf16[768,256]{1,0:T(8,128)(2,1)}, bf16[768,256]{1,0:T(8,128)(2,1)}) custom-call(s32[16]{0:T(128)S(1)} %copy-done.1, bf16[6,128,512]{2,1,0:T(8,128)(2,1)S(1)} %get-tuple-element.40.ext, bf16[128,512]{1,0:T(8,128)(2,1)S(1)} %collective-permute-done.7.late, ...), custom_call_target="tpu_custom_call" | custom-call | flops 100663296 | bytes 1720320 | tf_op jit(solution)/shard_map/pallas_call | solution.py:42
  63.8 1.1 %collective-permute-done.10.r2 = bf16[128,512]{1,0:T(8,128)(2,1)S(1)} collective-permute-done((bf16[128,512]{1,0:T(8,128)(2,1)S(1)}, bf16[128,512]{1,0:T(8,128)(2,1)S(1)}, u32[]{:S(2)}, u32[]{:S(2)}) %collective-permute-start.10) | collective-permute-done | bytes 131104 | tf_op jit(solution)/shard_map/ppermute | solution.py:19
  64.9 0.4 collective-permute-done.11.r3
  65.3 0.8 %shard_map.103 = bf16[128,2048]{1,0:T(8,128)(2,1)} custom-call(bf16[128,512]{1,0:T(8,128)(2,1)S(1)} %get-tuple-element.43.s0, bf16[128,512]{1,0:T(8,128)(2,1)S(1)} %collective-permute-done.9.r1, bf16[128,512]{1,0:T(8,128)(2,1)S(1)} %collective-permute-done.10.r2, bf16[128,512]{1,0:T(8,128)(2,1)S(1)} %collective-permute-done.11.r3), custom_call_target="tpu_custom_call" | custom-call | bytes 524288 | tf_op jit(solution)/shard_map/pallas_call | solution.py:42
  (13 shorter events, 0.0 us)
Async XLA Ops:
  0.6 6.6 %copy-start.2 = (s32[512]{0:T(512)S(1)}, s32[512]{0:T(512)}, u32[]{:S(2)}) copy-start(s32[512]{0:T(512)} %param.12) | copy-start | bytes 6148
  1.9 16.1 %collective-permute-start.2 = (bf16[64,4096]{1,0:T(8,128)(2,1)S(1)}, bf16[64,4096]{1,0:T(8,128)(2,1)S(1)}, u32[]{:S(2)}, u32[]{:S(2)}) collective-permute-start(bf16[64,4096]{1,0:T(8,128)(2,1)S(1)} %get-tuple-element.50.xa), channel_id=1, source_target_pairs={{0,1},{1,2},{2,3},{3,0},{4,5},{5,6},{6,7},{7,4},{8,9},{9,10},{10,1... | collective-permute-start | bytes 1572872 | tf_op jit(solution)/shard_map/ppermute | solution.py:19
  3.6 14.8 %collective-permute-start.1 = (bf16[64,4096]{1,0:T(8,128)(2,1)S(1)}, bf16[64,4096]{1,0:T(8,128)(2,1)S(1)}, u32[]{:S(2)}, u32[]{:S(2)}) collective-permute-start(bf16[64,4096]{1,0:T(8,128)(2,1)S(1)} %get-tuple-element.49.xb), channel_id=1, source_target_pairs={{0,3},{1,0},{2,1},{3,2},{4,7},{5,4},{6,5},{7,6},{8,11},{9,8},{10,9... | collective-permute-start | bytes 1572872 | tf_op jit(solution)/shard_map/ppermute | solution.py:19
  5.2 24.4 %collective-permute-start = (bf16[64,4096]{1,0:T(8,128)(2,1)S(1)}, bf16[64,4096]{1,0:T(8,128)(2,1)S(1)}, u32[]{:S(2)}, u32[]{:S(2)}) collective-permute-start(bf16[64,4096]{1,0:T(8,128)(2,1)S(1)} %get-tuple-element.50.xa), channel_id=1, source_target_pairs={{0,3},{1,0},{2,1},{3,2},{4,7},{5,4},{6,5},{7,6},{8,11},{9,8},{10,9... | collective-permute-start | bytes 1572872 | tf_op jit(solution)/shard_map/ppermute | solution.py:19
  7.0 22.6 %collective-permute-start.3 = (bf16[64,4096]{1,0:T(8,128)(2,1)S(1)}, bf16[64,4096]{1,0:T(8,128)(2,1)S(1)}, u32[]{:S(2)}, u32[]{:S(2)}) collective-permute-start(bf16[64,4096]{1,0:T(8,128)(2,1)S(1)} %get-tuple-element.49.xb), channel_id=1, source_target_pairs={{0,1},{1,2},{2,3},{3,0},{4,5},{5,6},{6,7},{7,4},{8,9},{9,10},{10,1... | collective-permute-start | bytes 1572872 | tf_op jit(solution)/shard_map/ppermute | solution.py:19
  18.0 26.3 %collective-permute-start.5 = (bf16[64,4096]{1,0:T(8,128)(2,1)S(1)}, bf16[64,4096]{1,0:T(8,128)(2,1)S(1)}, u32[]{:S(2)}, u32[]{:S(2)}) collective-permute-start(bf16[64,4096]{1,0:T(8,128)(2,1)S(1)} %collective-permute-done.2.la), channel_id=1, source_target_pairs={{0,1},{1,2},{2,3},{3,0},{4,5},{5,6},{6,7},{7,4},{8,9},{9,10},{10,1... | collective-permute-start | bytes 1572872 | tf_op jit(solution)/shard_map/ppermute | solution.py:19
  18.4 25.9 %collective-permute-start.6 = (bf16[64,4096]{1,0:T(8,128)(2,1)S(1)}, bf16[64,4096]{1,0:T(8,128)(2,1)S(1)}, u32[]{:S(2)}, u32[]{:S(2)}) collective-permute-start(bf16[64,4096]{1,0:T(8,128)(2,1)S(1)} %collective-permute-done.1.rb), channel_id=1, source_target_pairs={{0,3},{1,0},{2,1},{3,2},{4,7},{5,4},{6,5},{7,6},{8,11},{9,8},{10,9... | collective-permute-start | bytes 1572872 | tf_op jit(solution)/shard_map/ppermute | solution.py:19
  22.4 3.5 %copy-start = (f32[4096]{0:T(1024)S(1)}, f32[4096]{0:T(1024)}, u32[]{:S(2)}) copy-start(f32[4096]{0:T(1024)} %param.8) | copy-start | bytes 49156
  25.9 3.7 %copy-start.1 = (s32[16]{0:T(128)S(1)}, s32[16]{0:T(128)}, u32[]{:S(2)}) copy-start(s32[16]{0:T(128)} %owner.5) | copy-start | bytes 196
  32.1 11.2 %collective-permute-start.4 = (bf16[272,512]{1,0:T(8,128)(2,1)S(1)}, bf16[272,512]{1,0:T(8,128)(2,1)S(1)}, u32[]{:S(2)}, u32[]{:S(2)}) collective-permute-start(bf16[272,512]{1,0:T(8,128)(2,1)S(1)} %get-tuple-element.31), channel_id=1, source_target_pairs={{0,4},{1,5},{2,6},{3,7},{4,8},{5,9},{6,10},{7,11},{8,12},{9,13},{1... | collective-permute-start | bytes 835592 | tf_op jit(solution)/shard_map/ppermute | solution.py:25
  45.9 12.5 %collective-permute-start.7 = (bf16[128,512]{1,0:T(8,128)(2,1)S(1)}, bf16[128,512]{1,0:T(8,128)(2,1)S(1)}, u32[]{:S(2)}, u32[]{:S(2)}) collective-permute-start(bf16[128,512]{1,0:T(8,128)(2,1)S(1)} %get-tuple-element.38), channel_id=1, source_target_pairs={{0,4},{1,5},{4,8},{5,9},{6,2},{8,12},{9,13},{10,6},{12,16},{13,17}... | collective-permute-start | bytes 393224 | tf_op jit(solution)/shard_map/ppermute | solution.py:25
  47.8 14.3 %collective-permute-start.8 = (bf16[128,512]{1,0:T(8,128)(2,1)S(1)}, bf16[128,512]{1,0:T(8,128)(2,1)S(1)}, u32[]{:S(2)}, u32[]{:S(2)}) collective-permute-start(bf16[128,512]{1,0:T(8,128)(2,1)S(1)} %get-tuple-element.41), channel_id=1, source_target_pairs={{4,0},{5,1},{7,3},{8,4},{9,5},{11,7},{12,8},{13,9},{15,11},{16,12}... | collective-permute-start | bytes 393224 | tf_op jit(solution)/shard_map/ppermute | solution.py:25
  54.8 9.0 %collective-permute-start.9 = (bf16[128,512]{1,0:T(8,128)(2,1)S(1)}, bf16[128,512]{1,0:T(8,128)(2,1)S(1)}, u32[]{:S(2)}, u32[]{:S(2)}) collective-permute-start(bf16[128,512]{1,0:T(8,128)(2,1)S(1)} %get-tuple-element.44), channel_id=1, source_target_pairs={{0,1},{1,2},{2,3},{3,0},{4,5},{5,6},{6,7},{7,4},{8,9},{9,10},{10,1... | collective-permute-start | bytes 393224 | tf_op jit(solution)/shard_map/ppermute | solution.py:19
  58.3 6.6 %collective-permute-start.10 = (bf16[128,512]{1,0:T(8,128)(2,1)S(1)}, bf16[128,512]{1,0:T(8,128)(2,1)S(1)}, u32[]{:S(2)}, u32[]{:S(2)}) collective-permute-start(bf16[128,512]{1,0:T(8,128)(2,1)S(1)} %get-tuple-element.45), channel_id=1, source_target_pairs={{0,2},{1,3},{2,0},{3,1},{4,6},{5,7},{6,4},{7,5},{8,10},{9,11},{10,... | collective-permute-start | bytes 393224 | tf_op jit(solution)/shard_map/ppermute | solution.py:19
  59.5 5.8 %collective-permute-start.11 = (bf16[128,512]{1,0:T(8,128)(2,1)S(1)}, bf16[128,512]{1,0:T(8,128)(2,1)S(1)}, u32[]{:S(2)}, u32[]{:S(2)}) collective-permute-start(bf16[128,512]{1,0:T(8,128)(2,1)S(1)} %get-tuple-element.46), channel_id=1, source_target_pairs={{0,3},{1,0},{2,1},{3,2},{4,7},{5,4},{6,5},{7,6},{8,11},{9,8},{10,9... | collective-permute-start | bytes 393224 | tf_op jit(solution)/shard_map/ppermute | solution.py:19
